TPU v7x, 512 devices: a whole 4x4x16 slice. The times are simulated.
512 devices in a mesh: gx: 32 (over x_hi, z), gy: 16 (over x_lo, y, core).
Axes of the slice: x: 4 (x_hi: 2, x_lo: 2; x = x_hi * 2 + x_lo), y: 4, z: 16, core: 2. Of those that a mesh axis runs over, the one named last changes fastest.
Arguments:
- checkpoint: float32 [27, 8, 128, 2048], P(None, None, 'gx', 'gy'), may hold values from 0.0027 to 0.415, as said below
- rates: float32 [27], replicated, may hold values from 0.8 to 1.7
- wall_mask: int32 [8, 128, 2048], P(None, 'gx', 'gy'), may hold values 0 or 1
- cotangent: float32 [27, 8, 128, 2048], P(None, None, 'gx', 'gy'), may hold values from -6 to 6
Outputs:
- grad_checkpoint: float32 [27, 8, 128, 2048], P(None, None, 'gx', 'gy')
Inputs may be any that keep to these rules, and one draw needn't show every extreme that they name: `checkpoint`: each population lies between 0.6 and 1.4 times its lattice weight.
All inputs are finite; a program needn't handle non-finite values. No bound on the sum of `wall_mask` on one device may be relied on, other than what follows from the above.
Results may differ from a plain program's by a relative error of at most 0.00009.
Values sent between devices are 32-bit elements; how exact they have to be, the bound alone decides.
A program may use at most 64 MiB of HBM per device.

v0:
```python
import jax
import jax.numpy as jnp
import numpy as np
from jax import lax
from jax.sharding import PartitionSpec as P


def from_behind(block, axis, distance):
    devices = range(lax.axis_size(axis))
    route = [((i - distance) % len(devices), i) for i in devices]
    return lax.ppermute(block, axis, route)


def lattice_tables():
    signs = (-1, 0, 1)
    velocity = [[a, b, c] for a in signs for b in signs for c in signs]
    table = [8.0 / 27.0, 2.0 / 27.0, 1.0 / 54.0, 1.0 / 216.0]
    weights = [table[abs(a) + abs(b) + abs(c)] for a in signs for b in signs for c in signs]
    powers = [[1.0, 1.0, 1.0], [-1.0, 0.0, 1.0], [1.0, 0.0, 1.0]]
    undo = [[0.0, -0.5, 0.5], [1.0, 0.0, -1.0], [0.0, 0.5, 0.5]]
    moment = np.kron(np.kron(powers, powers), powers)
    inverse = np.kron(np.kron(undo, undo), undo)
    return (velocity, weights, moment, inverse)


def collide(incoming, rates, wall_cells):
    velocity, weights, moment, inverse = lattice_tables()
    velocity = jnp.asarray(velocity, jnp.float32)
    weights = jnp.asarray(weights, jnp.float32)
    moment = jnp.asarray(moment, jnp.float32)
    inverse = jnp.asarray(inverse, jnp.float32)
    high = lax.Precision.HIGHEST
    populations = incoming.reshape(27, -1)
    density = jnp.sum(populations, axis=0)
    momentum = jnp.dot(velocity.T, populations, precision=high)
    speeds = momentum / density
    projected = jnp.dot(velocity, speeds, precision=high)
    speed_sq = jnp.sum(speeds * speeds, axis=0)
    equilibrium = (
        weights[:, None]
        * density
        * (1.0 + 3.0 * projected + 4.5 * projected * projected - 1.5 * speed_sq)
    )
    relaxation = jnp.dot(inverse, rates[:, None] * moment, precision=high)
    collided = populations - jnp.dot(relaxation, populations - equilibrium, precision=high)
    reflected = populations[::-1]
    solid = wall_cells.reshape(1, -1)
    return (collided + solid * (reflected - collided)).reshape(incoming.shape)


def wall_field(wall_mask):
    height = lax.broadcasted_iota(jnp.int32, wall_mask.shape, 0)
    boundary = (height == 0) | (height == wall_mask.shape[0] - 1)
    return jnp.where(boundary, 1, wall_mask).astype(jnp.float32)


def stream(field, direction):
    planes, width_x, width_y = (field.shape[1], field.shape[2], field.shape[3])
    upper = 2 if direction > 0 else 0
    lower = 2 - upper
    lattice = field.reshape(3, 3, 3, planes, width_x, width_y)
    forward = lattice[upper]
    backward = lattice[lower]
    from_below = from_behind(forward[:, :, :, -1:, :], "gx", 1)
    from_above = from_behind(backward[:, :, :, :1, :], "gx", -1)
    forward = jnp.concatenate([from_below, forward[:, :, :, :-1, :]], axis=3)
    backward = jnp.concatenate([backward[:, :, :, 1:, :], from_above], axis=3)
    layers = [None, lattice[1], None]
    layers[upper] = forward
    layers[lower] = backward
    lattice = jnp.stack(layers)
    forward = lattice[:, upper]
    backward = lattice[:, lower]
    from_below = from_behind(forward[..., -1:], "gy", 1)
    from_above = from_behind(backward[..., :1], "gy", -1)
    forward = jnp.concatenate([from_below, forward[..., :-1]], axis=4)
    backward = jnp.concatenate([backward[..., 1:], from_above], axis=4)
    layers = [None, lattice[:, 1], None]
    layers[upper] = forward
    layers[lower] = backward
    lattice = jnp.stack(layers, axis=1)
    pieces = []
    for index_z in range(3):
        pieces.append(jnp.roll(lattice[:, :, index_z], direction * (index_z - 1), axis=2))
    return jnp.stack(pieces, axis=2).reshape(field.shape)


def shards(checkpoint, rates, wall_mask, cotangent):
    wall_cells = wall_field(wall_mask)
    back_one = stream(cotangent, -1)
    collided = collide(checkpoint, rates, wall_cells)
    next_state = stream(collided, 1)
    _, pullback = jax.vjp(lambda value: collide(value, rates, wall_cells), next_state)
    grad_next = pullback(back_one)[0]
    back_two = stream(grad_next, -1)
    _, pullback_first = jax.vjp(lambda value: collide(value, rates, wall_cells), checkpoint)
    return pullback_first(back_two)[0]


def solution(mesh):
    in_specs = (P(None, None, "gx", "gy"), P(), P(None, "gx", "gy"), P(None, None, "gx", "gy"))
    out_specs = P(None, None, "gx", "gy")
    return jax.shard_map(shards, mesh=mesh, in_specs=in_specs, out_specs=out_specs, check_vma=False)
```

profile of v0, /device:TPU:25, one launch (start us, length us, event | category | flops | bytes accessed | tf_op | source)
XLA Modules:
  0.0 85.3 jit_solution(98416090064480417)
XLA Ops:
  0.0 1.1 %fusion.68 = (f32[9,8,4,128]{3,2,1,0:T(4,128)S(1)}, f32[9,8,4,128]{3,2,1,0:T(4,128)S(1)}, f32[9,8,4,128]{3,2,1,0:T(4,128)S(1)}) fusion(f32[27,8,4,128]{3,2,1,0:T(4,128)} %param.19), kind=kLoop, calls=%fused_computation.143 | loop fusion | bytes 884736 | tf_op jit(solution)/shard_map/slice | solution.py:62
  1.2 13.6 %collective-permute-start.1 = (f32[3,3,8,1,128]{4,3,2,1,0:T(1,128)S(1)}, f32[3,3,8,1,128]{4,3,2,1,0:T(1,128)S(1)}, u32[]{:S(2)}, u32[]{:S(2)}) collective-permute-start(f32[3,3,8,1,128]{4,3,2,1,0:T(1,128)S(1)} %slice.277), channel_id=1, source_target_pairs={{16,0},{32,16},{48,32},{64,48},{80,64},{96,80},{112,96},{128,112},... | collective-permute-start | bytes 110600 | tf_op jit(solution)/shard_map/ppermute | solution.py:11
  14.8 1.9 %collective-permute-start = (f32[3,3,8,1,128]{4,3,2,1,0:T(1,128)S(1)}, f32[3,3,8,1,128]{4,3,2,1,0:T(1,128)S(1)}, u32[]{:S(2)}, u32[]{:S(2)}) collective-permute-start(f32[3,3,8,1,128]{4,3,2,1,0:T(1,128)S(1)} %slice.274), channel_id=1, source_target_pairs={{496,0},{0,16},{16,32},{32,48},{48,64},{64,80},{80,96},{96,112},{1... | collective-permute-start | bytes 110600 | tf_op jit(solution)/shard_map/ppermute | solution.py:11
  17.0 0.9 %rev.10 = f32[27,4096]{1,0:T(8,128)S(1)} reverse(f32[27,4096]{1,0:T(8,128)S(1)} %reshape.97), dimensions={0} | reverse | bytes 884736 | tf_op jit(solution)/shard_map/rev | solution.py:46
  18.3 0.6 fusion.64
  18.9 0.7 copy-done.2
  19.7 0.6 copy-done.4
  20.7 0.7 copy-done.3
  21.3 0.8 multiply_add_fusion
  22.3 7.0 %collective-permute-start.4 = (f32[3,3,8,1,128]{4,3,2,1,0:T(1,128)S(1)}, f32[3,3,8,1,128]{4,3,2,1,0:T(1,128)S(1)}, u32[]{:S(2)}, u32[]{:S(2)}) collective-permute-start(f32[3,3,8,1,128]{4,3,2,1,0:T(1,128)S(1)} %slice.294), channel_id=1, source_target_pairs={{16,0},{32,16},{48,32},{64,48},{80,64},{96,80},{112,96},{128,112},... | collective-permute-start | bytes 110600 | tf_op jit(solution)/shard_map/ppermute | solution.py:11
  29.4 1.9 %collective-permute-start.5 = (f32[3,3,8,1,128]{4,3,2,1,0:T(1,128)S(1)}, f32[3,3,8,1,128]{4,3,2,1,0:T(1,128)S(1)}, u32[]{:S(2)}, u32[]{:S(2)}) collective-permute-start(f32[3,3,8,1,128]{4,3,2,1,0:T(1,128)S(1)} %slice.297), channel_id=1, source_target_pairs={{496,0},{0,16},{16,32},{32,48},{48,64},{64,80},{80,96},{96,112},{1... | collective-permute-start | bytes 110600 | tf_op jit(solution)/shard_map/ppermute | solution.py:11
  32.1 3.3 %collective-permute-start.2 = (f32[3,3,8,4,1]{4,3,2,0,1:T(4,128)S(1)}, f32[3,3,8,4,1]{4,3,2,0,1:T(4,128)S(1)}, u32[]{:S(2)}, u32[]{:S(2)}) collective-permute-start(f32[3,3,8,4,1]{4,3,2,0,1:T(4,128)S(1)} %slice.279), channel_id=1, source_target_pairs={{15,0},{0,1},{1,2},{2,3},{3,4},{4,5},{5,6},{6,7},{7,8},{8,9},{9,10... | collective-permute-start | bytes 3464 | tf_op jit(solution)/shard_map/ppermute | solution.py:11
  35.5 2.1 %collective-permute-start.3 = (f32[3,3,8,4,1]{4,3,2,0,1:T(4,128)S(1)}, f32[3,3,8,4,1]{4,3,2,0,1:T(4,128)S(1)}, u32[]{:S(2)}, u32[]{:S(2)}) collective-permute-start(f32[3,3,8,4,1]{4,3,2,0,1:T(4,128)S(1)} %bitcast.147), channel_id=1, source_target_pairs={{1,0},{2,1},{3,2},{4,3},{5,4},{6,5},{7,6},{8,7},{9,8},{10,9},{11,1... | collective-permute-start | bytes 3464 | tf_op jit(solution)/shard_map/ppermute | solution.py:11
  38.1 4.7 %collective-permute-start.6 = (f32[3,3,8,4,1]{4,3,2,0,1:T(4,128)S(1)}, f32[3,3,8,4,1]{4,3,2,0,1:T(4,128)S(1)}, u32[]{:S(2)}, u32[]{:S(2)}) collective-permute-start(f32[3,3,8,4,1]{4,3,2,0,1:T(4,128)S(1)} %bitcast.148), channel_id=1, source_target_pairs={{1,0},{2,1},{3,2},{4,3},{5,4},{6,5},{7,6},{8,7},{9,8},{10,9},{11,1... | collective-permute-start | bytes 3464 | tf_op jit(solution)/shard_map/ppermute | solution.py:11
  43.0 3.0 %collective-permute-start.7 = (f32[3,3,8,4,1]{4,3,2,0,1:T(4,128)S(1)}, f32[3,3,8,4,1]{4,3,2,0,1:T(4,128)S(1)}, u32[]{:S(2)}, u32[]{:S(2)}) collective-permute-start(f32[3,3,8,4,1]{4,3,2,0,1:T(4,128)S(1)} %slice.304), channel_id=1, source_target_pairs={{15,0},{0,1},{1,2},{2,3},{3,4},{4,5},{5,6},{6,7},{7,8},{8,9},{9,10... | collective-permute-start | bytes 3464 | tf_op jit(solution)/shard_map/ppermute | solution.py:11
  46.9 1.1 %collective-permute-done.7 = f32[3,3,8,4,1]{4,3,2,0,1:T(4,128)S(1)} collective-permute-done((f32[3,3,8,4,1]{4,3,2,0,1:T(4,128)S(1)}, f32[3,3,8,4,1]{4,3,2,0,1:T(4,128)S(1)}, u32[]{:S(2)}, u32[]{:S(2)}) %collective-permute-start.7) | collective-permute-done | bytes 1184 | tf_op jit(solution)/shard_map/ppermute | solution.py:11
  49.7 0.6 fusion.65
  50.4 0.8 fusion.29
  51.2 0.9 %rev.9 = f32[27,4096]{1,0:T(8,128)S(1)} reverse(f32[27,4096]{1,0:T(8,128)S(1)} %broadcast_multiply_fusion.1), dimensions={0} | reverse | bytes 884736 | tf_op jit(solution)/shard_map/transpose(jvp())/rev | solution.py:46
  52.1 0.6 multiply_reduce_fusion.2
  52.7 0.6 fusion.1
  53.5 1.9 %collective-permute-start.8 = (f32[3,3,8,1,128]{4,3,2,1,0:T(1,128)S(1)}, f32[3,3,8,1,128]{4,3,2,1,0:T(1,128)S(1)}, u32[]{:S(2)}, u32[]{:S(2)}) collective-permute-start(f32[3,3,8,1,128]{4,3,2,1,0:T(1,128)S(1)} %slice.314), channel_id=1, source_target_pairs={{496,0},{0,16},{16,32},{32,48},{48,64},{64,80},{80,96},{96,112},{1... | collective-permute-start | bytes 110600 | tf_op jit(solution)/shard_map/ppermute | solution.py:11
  55.7 7.6 %collective-permute-start.9 = (f32[3,3,8,1,128]{4,3,2,1,0:T(1,128)S(1)}, f32[3,3,8,1,128]{4,3,2,1,0:T(1,128)S(1)}, u32[]{:S(2)}, u32[]{:S(2)}) collective-permute-start(f32[3,3,8,1,128]{4,3,2,1,0:T(1,128)S(1)} %slice.319), channel_id=1, source_target_pairs={{16,0},{32,16},{48,32},{64,48},{80,64},{96,80},{112,96},{128,112},... | collective-permute-start | bytes 110600 | tf_op jit(solution)/shard_map/ppermute | solution.py:11
  63.5 0.8 collective-permute-done.9
  64.7 7.0 %collective-permute-start.10 = (f32[3,3,8,4,1]{4,3,2,0,1:T(4,128)S(1)}, f32[3,3,8,4,1]{4,3,2,0,1:T(4,128)S(1)}, u32[]{:S(2)}, u32[]{:S(2)}) collective-permute-start(f32[3,3,8,4,1]{4,3,2,0,1:T(4,128)S(1)} %slice.321), channel_id=1, source_target_pairs={{15,0},{0,1},{1,2},{2,3},{3,4},{4,5},{5,6},{6,7},{7,8},{8,9},{9,10... | collective-permute-start | bytes 3464 | tf_op jit(solution)/shard_map/ppermute | solution.py:11
  71.9 2.1 %collective-permute-start.11 = (f32[3,3,8,4,1]{4,3,2,0,1:T(4,128)S(1)}, f32[3,3,8,4,1]{4,3,2,0,1:T(4,128)S(1)}, u32[]{:S(2)}, u32[]{:S(2)}) collective-permute-start(f32[3,3,8,4,1]{4,3,2,0,1:T(4,128)S(1)} %bitcast.149), channel_id=1, source_target_pairs={{1,0},{2,1},{3,2},{4,3},{5,4},{6,5},{7,6},{8,7},{9,8},{10,9},{11,1... | collective-permute-start | bytes 3464 | tf_op jit(solution)/shard_map/ppermute | solution.py:11
  74.1 6.3 %collective-permute-done.11 = f32[3,3,8,4,1]{4,3,2,0,1:T(4,128)S(1)} collective-permute-done((f32[3,3,8,4,1]{4,3,2,0,1:T(4,128)S(1)}, f32[3,3,8,4,1]{4,3,2,0,1:T(4,128)S(1)}, u32[]{:S(2)}, u32[]{:S(2)}) %collective-permute-start.11) | collective-permute-done | bytes 1184 | tf_op jit(solution)/shard_map/ppermute | solution.py:11
  81.2 0.8 fusion.30
  82.1 0.9 %rev.11 = f32[27,4096]{1,0:T(8,128)S(1)} reverse(f32[27,4096]{1,0:T(8,128)S(1)} %broadcast_multiply_fusion), dimensions={0} | reverse | bytes 884736 | tf_op jit(solution)/shard_map/transpose(jvp())/rev | solution.py:46
  83.0 0.6 multiply_reduce_fusion.1
  83.6 0.6 fusion
  84.2 1.1 %reshape.98 = f32[27,8,4,128]{3,2,1,0:T(4,128)} reshape(f32[27,4096]{1,0:T(8,128)S(1)} %fusion) | data formatting | bytes 884736 | tf_op jit(solution)/shard_map/transpose(jvp())/reshape | solution.py:33
  (107 shorter events, 7.4 us)
Async XLA Ops:
  0.0 16.8 %copy-start = (f32[27,8,4,128]{3,2,1,0:T(4,128)S(1)}, f32[27,8,4,128]{3,2,1,0:T(4,128)}, u32[]{:S(2)}) copy-start(f32[27,8,4,128]{3,2,1,0:T(4,128)} %param.16) | copy-start | bytes 1327108
  1.2 30.4 %collective-permute-start.1 = (f32[3,3,8,1,128]{4,3,2,1,0:T(1,128)S(1)}, f32[3,3,8,1,128]{4,3,2,1,0:T(1,128)S(1)}, u32[]{:S(2)}, u32[]{:S(2)}) collective-permute-start(f32[3,3,8,1,128]{4,3,2,1,0:T(1,128)S(1)} %slice.277), channel_id=1, source_target_pairs={{16,0},{32,16},{48,32},{64,48},{80,64},{96,80},{112,96},{128,112},... | collective-permute-start | bytes 110600 | tf_op jit(solution)/shard_map/ppermute | solution.py:11
  14.8 16.9 %collective-permute-start = (f32[3,3,8,1,128]{4,3,2,1,0:T(1,128)S(1)}, f32[3,3,8,1,128]{4,3,2,1,0:T(1,128)S(1)}, u32[]{:S(2)}, u32[]{:S(2)}) collective-permute-start(f32[3,3,8,1,128]{4,3,2,1,0:T(1,128)S(1)} %slice.274), channel_id=1, source_target_pairs={{496,0},{0,16},{16,32},{32,48},{48,64},{64,80},{80,96},{96,112},{1... | collective-permute-start | bytes 110600 | tf_op jit(solution)/shard_map/ppermute | solution.py:11
  17.0 0.9 %copy-start.1 = (f32[27,3]{1,0:T(8,128)S(1)}, f32[27,3]{1,0:T(8,128)}, u32[]{:S(2)}) copy-start(f32[27,3]{1,0:T(8,128)} %constant.11.clone) | copy-start | bytes 976
  18.9 0.7 copy-start.2
  19.6 0.7 copy-start.4
  19.6 0.7 copy-start.5
  19.6 0.7 copy-start.6
  20.6 0.7 copy-start.3
  22.3 15.3 %collective-permute-start.4 = (f32[3,3,8,1,128]{4,3,2,1,0:T(1,128)S(1)}, f32[3,3,8,1,128]{4,3,2,1,0:T(1,128)S(1)}, u32[]{:S(2)}, u32[]{:S(2)}) collective-permute-start(f32[3,3,8,1,128]{4,3,2,1,0:T(1,128)S(1)} %slice.294), channel_id=1, source_target_pairs={{16,0},{32,16},{48,32},{64,48},{80,64},{96,80},{112,96},{128,112},... | collective-permute-start | bytes 110600 | tf_op jit(solution)/shard_map/ppermute | solution.py:11
  29.4 8.3 %collective-permute-start.5 = (f32[3,3,8,1,128]{4,3,2,1,0:T(1,128)S(1)}, f32[3,3,8,1,128]{4,3,2,1,0:T(1,128)S(1)}, u32[]{:S(2)}, u32[]{:S(2)}) collective-permute-start(f32[3,3,8,1,128]{4,3,2,1,0:T(1,128)S(1)} %slice.297), channel_id=1, source_target_pairs={{496,0},{0,16},{16,32},{32,48},{48,64},{64,80},{80,96},{96,112},{1... | collective-permute-start | bytes 110600 | tf_op jit(solution)/shard_map/ppermute | solution.py:11
  32.1 13.9 %collective-permute-start.2 = (f32[3,3,8,4,1]{4,3,2,0,1:T(4,128)S(1)}, f32[3,3,8,4,1]{4,3,2,0,1:T(4,128)S(1)}, u32[]{:S(2)}, u32[]{:S(2)}) collective-permute-start(f32[3,3,8,4,1]{4,3,2,0,1:T(4,128)S(1)} %slice.279), channel_id=1, source_target_pairs={{15,0},{0,1},{1,2},{2,3},{3,4},{4,5},{5,6},{6,7},{7,8},{8,9},{9,10... | collective-permute-start | bytes 3464 | tf_op jit(solution)/shard_map/ppermute | solution.py:11
  35.5 10.6 %collective-permute-start.3 = (f32[3,3,8,4,1]{4,3,2,0,1:T(4,128)S(1)}, f32[3,3,8,4,1]{4,3,2,0,1:T(4,128)S(1)}, u32[]{:S(2)}, u32[]{:S(2)}) collective-permute-start(f32[3,3,8,4,1]{4,3,2,0,1:T(4,128)S(1)} %bitcast.147), channel_id=1, source_target_pairs={{1,0},{2,1},{3,2},{4,3},{5,4},{6,5},{7,6},{8,7},{9,8},{10,9},{11,1... | collective-permute-start | bytes 3464 | tf_op jit(solution)/shard_map/ppermute | solution.py:11
  38.1 8.6 %collective-permute-start.6 = (f32[3,3,8,4,1]{4,3,2,0,1:T(4,128)S(1)}, f32[3,3,8,4,1]{4,3,2,0,1:T(4,128)S(1)}, u32[]{:S(2)}, u32[]{:S(2)}) collective-permute-start(f32[3,3,8,4,1]{4,3,2,0,1:T(4,128)S(1)} %bitcast.148), channel_id=1, source_target_pairs={{1,0},{2,1},{3,2},{4,3},{5,4},{6,5},{7,6},{8,7},{9,8},{10,9},{11,1... | collective-permute-start | bytes 3464 | tf_op jit(solution)/shard_map/ppermute | solution.py:11
  43.0 5.1 %collective-permute-start.7 = (f32[3,3,8,4,1]{4,3,2,0,1:T(4,128)S(1)}, f32[3,3,8,4,1]{4,3,2,0,1:T(4,128)S(1)}, u32[]{:S(2)}, u32[]{:S(2)}) collective-permute-start(f32[3,3,8,4,1]{4,3,2,0,1:T(4,128)S(1)} %slice.304), channel_id=1, source_target_pairs={{15,0},{0,1},{1,2},{2,3},{3,4},{4,5},{5,6},{6,7},{7,8},{8,9},{9,10... | collective-permute-start | bytes 3464 | tf_op jit(solution)/shard_map/ppermute | solution.py:11
  53.5 9.9 %collective-permute-start.8 = (f32[3,3,8,1,128]{4,3,2,1,0:T(1,128)S(1)}, f32[3,3,8,1,128]{4,3,2,1,0:T(1,128)S(1)}, u32[]{:S(2)}, u32[]{:S(2)}) collective-permute-start(f32[3,3,8,1,128]{4,3,2,1,0:T(1,128)S(1)} %slice.314), channel_id=1, source_target_pairs={{496,0},{0,16},{16,32},{32,48},{48,64},{64,80},{80,96},{96,112},{1... | collective-permute-start | bytes 110600 | tf_op jit(solution)/shard_map/ppermute | solution.py:11
  55.7 8.7 %collective-permute-start.9 = (f32[3,3,8,1,128]{4,3,2,1,0:T(1,128)S(1)}, f32[3,3,8,1,128]{4,3,2,1,0:T(1,128)S(1)}, u32[]{:S(2)}, u32[]{:S(2)}) collective-permute-start(f32[3,3,8,1,128]{4,3,2,1,0:T(1,128)S(1)} %slice.319), channel_id=1, source_target_pairs={{16,0},{32,16},{48,32},{64,48},{80,64},{96,80},{112,96},{128,112},... | collective-permute-start | bytes 110600 | tf_op jit(solution)/shard_map/ppermute | solution.py:11
  64.7 9.2 %collective-permute-start.10 = (f32[3,3,8,4,1]{4,3,2,0,1:T(4,128)S(1)}, f32[3,3,8,4,1]{4,3,2,0,1:T(4,128)S(1)}, u32[]{:S(2)}, u32[]{:S(2)}) collective-permute-start(f32[3,3,8,4,1]{4,3,2,0,1:T(4,128)S(1)} %slice.321), channel_id=1, source_target_pairs={{15,0},{0,1},{1,2},{2,3},{3,4},{4,5},{5,6},{6,7},{7,8},{8,9},{9,10... | collective-permute-start | bytes 3464 | tf_op jit(solution)/shard_map/ppermute | solution.py:11
  71.9 8.6 %collective-permute-start.11 = (f32[3,3,8,4,1]{4,3,2,0,1:T(4,128)S(1)}, f32[3,3,8,4,1]{4,3,2,0,1:T(4,128)S(1)}, u32[]{:S(2)}, u32[]{:S(2)}) collective-permute-start(f32[3,3,8,4,1]{4,3,2,0,1:T(4,128)S(1)} %bitcast.149), channel_id=1, source_target_pairs={{1,0},{2,1},{3,2},{4,3},{5,4},{6,5},{7,6},{8,7},{9,8},{10,9},{11,1... | collective-permute-start | bytes 3464 | tf_op jit(solution)/shard_map/ppermute | solution.py:11
where the time goes:
time: 85.9 us; the launch traced here: 85.3 us
  starting transfers between devices  56 us (65%)
  local copies, waits for them, and re-layouts  9.71 us (11%)
  waiting for transfers between devices  8.63 us (10%)
  matrix products  7.04 us (8%)
  other arithmetic  2.96 us (3%)
  between operations  0.91 us (1%)
    ppermute x12, starting transfers between devices, from_behind(): return lax.ppermute(block, axis, route)  56 us
    ppermute x12, waiting for transfers between devices, from_behind(): return lax.ppermute(block, axis, route)  8.63 us
    rev x3, local copies, waits for them, and re-layouts, collide(): reflected = populations[::-1]  2.58 us
    dot_general x3, matrix products, collide(): jnp.dot(relaxation, populations - equilibrium, precision=high)  2.39 us
    dot_general x4, matrix products, collide(): projected = jnp.dot(velocity, speeds, precision=high)  2.36 us
    unnamed x14, local copies, waits for them, and re-layouts  2.05 us
    dot_general x4, matrix products, collide(): momentum = jnp.dot(velocity.T, populations, precision=high)  2.02 us
  transfers between devices with their start and end apart: 12, of which 5 were waited for; matrix products, arithmetic and copies ran while one was open for 7% of the time, Pallas kernels for 0%

commit v1 on v0

v1 whole, which is shorter than its diff:
```python
import functools

import jax
import jax.numpy as jnp
from jax import lax
from jax.experimental import pallas as pl
from jax.experimental.pallas import tpu as pltpu
from jax.sharding import PartitionSpec as P

F32 = jnp.float32
MESH = pl.DeviceIdType.MESH
ROWS = 4
Q = [(a, b, c) for a in (-1, 0, 1) for b in (-1, 0, 1) for c in (-1, 0, 1)]
THIRD = 1.0 / 3.0
NINTH = 1.0 / 9.0


def rollz(v, s):
    return v if s == 0 else pltpu.roll(v, s % 8, 0)


def rolly(v, s):
    return v if s % 128 == 0 else pltpu.roll(v, s % 128, 1)


def lanes():
    return lax.broadcasted_iota(jnp.int32, (8, 128), 1)


def along(values, axis, fn):
    out = [None] * 27
    step = (9, 3, 1)[axis]
    for i in range(27):
        if (i // step) % 3 == 0:
            out[i], out[i + step], out[i + 2 * step] = fn(
                values[i], values[i + step], values[i + 2 * step]
            )
    return out


def to_moments(a, b, c):
    s = a + c
    return s + b, c - a, s


def from_halved(m0, m1, m2):
    a, c = m2 - m1, m2 + m1
    return a, m0 - (a + c), c


def dual_doubled(a, b, c):
    return b, c - a, (a + c) - (b + b)


def dual_back(m0, m1, m2):
    s = m0 + m2
    return s - m1, m0, s + m1


def at(i, j, k):
    return 9 * i + 3 * j + k


def halved_rates(rates_ref):
    return [
        rates_ref[0, n] * (0.5 ** sum(p > 0 for p in (n // 9, n // 3 % 3, n % 3)))
        for n in range(27)
    ]


def collide(f, rates, wall):
    m = f
    for axis in (2, 1, 0):
        m = along(m, axis, to_moments)
    rho, jx, jy, jz = m[0], m[9], m[3], m[1]
    inv = 1.0 / rho
    ux, uy, uz = jx * inv, jy * inv, jz * inv
    xx, yy, zz = jx * ux, jy * uy, jz * uz
    xy, xz, yz = jx * uy, jx * uz, jy * uz
    r3, r9 = rho * THIRD, rho * NINTH
    x3, y3, z3 = jx * THIRD, jy * THIRD, jz * THIRD
    eq = [None] * 27
    eq[at(0, 0, 0)] = rho
    eq[at(1, 0, 0)], eq[at(0, 1, 0)], eq[at(0, 0, 1)] = jx, jy, jz
    eq[at(2, 0, 0)], eq[at(0, 2, 0)], eq[at(0, 0, 2)] = r3 + xx, r3 + yy, r3 + zz
    eq[at(1, 1, 0)], eq[at(1, 0, 1)], eq[at(0, 1, 1)] = xy, xz, yz
    eq[at(1, 2, 0)] = eq[at(1, 0, 2)] = x3
    eq[at(2, 1, 0)] = eq[at(0, 1, 2)] = y3
    eq[at(2, 0, 1)] = eq[at(0, 2, 1)] = z3
    eq[at(1, 2, 2)], eq[at(2, 1, 2)], eq[at(2, 2, 1)] = x3 * THIRD, y3 * THIRD, z3 * THIRD
    eq[at(1, 1, 2)], eq[at(1, 2, 1)], eq[at(2, 1, 1)] = xy * THIRD, xz * THIRD, yz * THIRD
    eq[at(2, 2, 0)] = r9 + (xx + yy) * THIRD
    eq[at(2, 0, 2)] = r9 + (xx + zz) * THIRD
    eq[at(0, 2, 2)] = r9 + (yy + zz) * THIRD
    eq[at(2, 2, 2)] = r9 * THIRD + (xx + yy + zz) * NINTH
    d = [
        m[n] * rates[n] if eq[n] is None else (m[n] - eq[n]) * rates[n]
        for n in range(27)
    ]
    for axis in (0, 1, 2):
        d = along(d, axis, from_halved)
    solid = wall > 0.5
    out = [jnp.where(solid, f[26 - n], f[n] - d[n]) for n in range(27)]
    return out, (ux, uy, uz)


def pull_back(g, u, rates, wall, keep=range(27)):
    ux, uy, uz = u
    e = g
    for axis in (2, 1, 0):
        e = along(e, axis, dual_doubled)
    e = [e[n] * rates[n] for n in range(27)]
    e222 = e[at(2, 2, 2)] * NINTH
    pair_xy, pair_xz, pair_yz = e[at(2, 2, 0)], e[at(2, 0, 2)], e[at(0, 2, 2)]
    pxx = e[at(2, 0, 0)] + (pair_xy + pair_xz) * THIRD + e222
    pyy = e[at(0, 2, 0)] + (pair_xy + pair_yz) * THIRD + e222
    pzz = e[at(0, 0, 2)] + (pair_xz + pair_yz) * THIRD + e222
    pxy = e[at(1, 1, 0)] + e[at(1, 1, 2)] * THIRD
    pxz = e[at(1, 0, 1)] + e[at(1, 2, 1)] * THIRD
    pyz = e[at(0, 1, 1)] + e[at(2, 1, 1)] * THIRD
    rho = (
        e[0]
        + (e[at(2, 0, 0)] + e[at(0, 2, 0)] + e[at(0, 0, 2)] + e222) * THIRD
        + (pair_xy + pair_xz + pair_yz) * NINTH
    )
    cx = e[at(1, 0, 0)] + (e[at(1, 2, 0)] + e[at(1, 0, 2)]) * THIRD + e[at(1, 2, 2)] * NINTH
    cy = e[at(0, 1, 0)] + (e[at(2, 1, 0)] + e[at(0, 1, 2)]) * THIRD + e[at(2, 1, 2)] * NINTH
    cz = e[at(0, 0, 1)] + (e[at(2, 0, 1)] + e[at(0, 2, 1)]) * THIRD + e[at(2, 2, 1)] * NINTH
    sx = (pxx + pxx) * ux + pxy * uy + pxz * uz
    sy = (pyy + pyy) * uy + pxy * ux + pyz * uz
    sz = (pzz + pzz) * uz + pxz * ux + pyz * uy
    rho = rho - 0.5 * (ux * sx + uy * sy + uz * sz)
    e[at(0, 0, 0)] = e[at(0, 0, 0)] - rho
    e[at(1, 0, 0)] = e[at(1, 0, 0)] - (cx + sx)
    e[at(0, 1, 0)] = e[at(0, 1, 0)] - (cy + sy)
    e[at(0, 0, 1)] = e[at(0, 0, 1)] - (cz + sz)
    for axis in (2, 1, 0):
        e = along(e, axis, dual_back)
    solid = wall > 0.5
    return {n: jnp.where(solid, g[26 - n], g[n] - e[n]) for n in keep}


def row(ref, q, x):
    return ref[pl.ds(q * 32 + x, 8, stride=4), :]


def wall_row(ref, x):
    height = lax.broadcasted_iota(jnp.int32, (8, 128), 0)
    mask = ref[pl.ds(x, 8, stride=4), :]
    return jnp.where((height == 0) | (height == 7), 1, mask).astype(F32)


def prepare(ck, cot, wall, rates_ref, sxc, mb, ey, uck):
    lane = lanes()
    rates = halved_rates(rates_ref)
    for q in range(18):
        sxc[1, q] = row(cot, q, 3)
        sxc[0, q] = row(cot, q + 9, 0)
    for q in range(9):
        sxc[1, 18 + q] = row(cot, q, 2)
        sxc[0, 18 + q] = row(cot, q + 18, 1)

    zero = jnp.zeros((8, 128), F32)
    first, last = lane == 0, lane == 127
    body = [[zero] * 4 for _ in range(6)]
    edge = [[zero] * 3 for _ in range(6)]
    for x in range(ROWS):
        w = wall_row(wall, x)
        mb[x + 1, 4] = w
        out, u = collide([row(ck, q, x) for q in range(27)], rates, w)
        for k in range(3):
            uck[x, k] = u[k]
        for a in range(3):
            sums, tilts = [], []
            for b in range(3):
                up = rollz(out[at(a, b, 2)], 1)
                down = rollz(out[at(a, b, 0)], -1)
                sums.append(out[at(a, b, 1)] + (up + down))
                tilts.append(up - down)
            ap, am = rolly(sums[2], 1), rolly(sums[0], -1)
            bp, bm = rolly(tilts[2], 1), rolly(tilts[0], -1)
            r = x + a
            outer = jnp.where(first, ap, am)
            edge[r][0] = edge[r][0] + outer
            edge[r][1] = edge[r][1] + (a - 1) * outer if a != 1 else edge[r][1]
            edge[r][2] = edge[r][2] + jnp.where(first, bp, bm)
            ap, am = jnp.where(first, 0.0, ap), jnp.where(last, 0.0, am)
            bp, bm = jnp.where(first, 0.0, bp), jnp.where(last, 0.0, bm)
            total = sums[1] + (ap + am)
            body[r][0] = body[r][0] + total
            if a != 1:
                body[r][1] = body[r][1] + (a - 1) * total
            body[r][2] = body[r][2] + (ap - am)
            body[r][3] = body[r][3] + (tilts[1] + (bp + bm))
    for r in range(6):
        for k in range(4):
            mb[r, k] = body[r][k]
    mb[0, 4] = zero
    mb[5, 4] = zero

    r0, r1, r2, l0, l1, l2, l0m = [zero] * 7
    for i, (cx, cz) in enumerate([(a, c) for a in range(3) for c in range(3)]):
        for x in range(ROWS):
            d = 8 * i + x + 2
            here, before, after = lane == d, lane == d - 1, lane == d + 1
            v = rolly(row(cot, at(cx, 0, cz), x), d - 127)
            r0, r2 = jnp.where(here, v, r0), jnp.where(before, v, r2)
            v = rolly(row(cot, at(cx, 2, cz), x), d)
            l0, l2 = jnp.where(here, v, l0), jnp.where(after, v, l2)
            v = rolly(row(cot, at(cx, 1, cz), x), d - 127)
            r1, l1 = jnp.where(here, v, r1), jnp.where(after, v, l1)
    for r in range(6):
        outer = edge[r]
        outer = [outer[0], outer[1], jnp.where(first, outer[0], -outer[0]), outer[2]]
        for k in range(4):
            d = 8 * (9 + k) + r + 1
            here, before, after = lane == d, lane == d - 1, lane == d + 1
            v = rolly(body[r][k], d - 127)
            r1, l1 = jnp.where(here, v, r1), jnp.where(after, v, l1)
            v = rolly(outer[k], d)
            r0, l0m = jnp.where(here, v, r0), jnp.where(before, v, l0m)
    for x in range(ROWS):
        d = 8 * 13 + x + 2
        v = rolly(wall_row(wall, x), d - 127)
        r1, l1 = jnp.where(lane == d, v, r1), jnp.where(lane == d + 1, v, l1)
    ey[0, 0] = l0 + rolly(l0m, 1)
    ey[1, 0] = rolly(l1, -1)
    ey[2, 0] = rolly(l2, -1)
    ey[0, 1] = r0
    ey[1, 1] = r1
    ey[2, 1] = rolly(r2, 1)


def exchange(sizes, sxc, mb, ey, xc, xm, xe, en, send, recv):
    nx, ny = sizes

    def device(dx, dy):
        return (
            lax.rem(lax.axis_index("gx") + (dx + nx), nx),
            lax.rem(lax.axis_index("gy") + (dy + ny), ny),
        )

    around = [(a, b) for a in (1, 0, -1) for b in (1, 0, -1) if (a, b) != (0, 0)]
    barrier = pltpu.get_barrier_semaphore()
    for d in around:
        pl.semaphore_signal(barrier, inc=1, device_id=device(*d), device_id_type=MESH)
    pl.semaphore_wait(barrier, 8)
    copies = []

    def put(src, dst, dx, dy):
        n = len(copies)
        copies.append(
            pltpu.make_async_remote_copy(
                src_ref=src,
                dst_ref=dst,
                send_sem=send.at[n],
                recv_sem=recv.at[n],
                device_id=device(dx, dy),
                device_id_type=MESH,
            )
        )
        copies[-1].start()

    put(ey.at[:, 1], en.at[1], 1, 1)
    put(ey.at[:, 0], en.at[4], 1, -1)
    put(mb.at[pl.ds(4, 2)], xm.at[0], 1, 0)
    put(ey.at[0], xe.at[0], 1, 0)
    put(sxc.at[1], xc.at[0], 1, 0)
    put(ey.at[:, 1], en.at[2], -1, 1)
    put(ey.at[:, 0], en.at[5], -1, -1)
    put(mb.at[pl.ds(0, 2)], xm.at[1], -1, 0)
    put(ey.at[0], xe.at[1], -1, 0)
    put(sxc.at[0], xc.at[1], -1, 0)
    put(ey.at[:, 1], en.at[0], 0, 1)
    put(ey.at[:, 0], en.at[3], 0, -1)
    for c in copies:
        c.wait_recv()
    for c in copies:
        c.wait_send()


def finish(cot, wall, rates_ref, mb, ey, uck, xc, xm, xe, en, out, gn, gy):
    lane = lanes()
    rates = halved_rates(rates_ref)
    first, last = lane == 0, lane == 127
    low, high = lane % 8 < 3, lane % 8 >= 5
    left = lane < 8

    def merge(own, below, above):
        below, above = rolly(below, -4), rolly(above, 4)
        return own + jnp.where(low, below, 0.0) + jnp.where(high, above, 0.0)

    exl = [merge(en[0, k], en[1, k], en[2, k]) for k in range(3)]
    exr = [merge(en[3, k], en[4, k], en[5, k]) for k in range(3)]
    oxl = merge(ey[0, 0], xe[0, 0], xe[1, 0])
    oxr = merge(ey[0, 1], xe[0, 1], xe[1, 1])

    def source(q, x):
        if 0 <= x < ROWS:
            return row(cot, q, x)
        if x == -1:
            return xc[0, q]
        if x == -2:
            return xc[0, 18 + q]
        return xc[1, q - 9] if x == ROWS else xc[1, q]

    def slot(q):
        return 3 * (q // 9) + q % 3

    g = []
    for q, (cx, cy, cz) in enumerate(Q):
        s = slot(q)
        lo, hi = ((exl[2], oxr), (exl[1], exr[1]), (oxl, exr[2]))[cy + 1]
        v = jnp.where(left, rolly(lo, -8 * s - cx), rolly(hi, 8 - 8 * s - cx))
        g.append(rollz(v, -cz))
    m = []
    for k in range(4):
        s = 9 + k
        lo, hi = exl[1] + oxl, exr[1] + oxr
        m.append(jnp.where(left, rolly(lo, -8 * s), rolly(hi, 8 - 8 * s)))
    w = jnp.where(left, rolly(exl[1], -104), rolly(exr[1], -96))
    inv = 1.0 / jnp.where((lane < 16) & (lane % 8 > 0) & (lane % 8 < 7), m[0], 1.0)
    got = pull_back(g, [m[k] * inv for k in (1, 2, 3)], rates, w)
    for q, (cx, cy, cz) in enumerate(Q):
        if cy != 0:
            gy[q] = got[q]

    for x in range(-1, ROWS + 1):
        m = []
        for k in range(4):
            v = mb[x + 1, k]
            if x <= 0:
                v = v + xm[0, x + 1, k]
            if x >= 3:
                v = v + xm[1, x - 3, k]
            d = 8 * (9 + k) + x + 2
            v = v + jnp.where(first, rolly(exl[0], -d), 0.0)
            v = v + jnp.where(last, rolly(exr[0], 127 - d), 0.0)
            m.append(v)
        w = xm[0, 0, 4] if x < 0 else xm[1, 1, 4] if x == ROWS else wall_row(wall, x)
        g = []
        for q, (cx, cy, cz) in enumerate(Q):
            v = source(q, x + cx)
            d = 8 * slot(q) + x + cx + 2
            if cy == 1:
                v = jnp.where(last, rolly(exr[0], 127 - d), rolly(v, -1))
            if cy == -1:
                v = jnp.where(first, rolly(exl[0], -d), rolly(v, 1))
            g.append(rollz(v, -cz))
        inv = 1.0 / m[0]
        keep = range(9) if x < 0 else range(18, 27) if x == ROWS else range(27)
        got = pull_back(g, [m[k] * inv for k in (1, 2, 3)], rates, w, keep)
        for q in keep:
            gn[x + 1, q] = got[q]

    for x in range(ROWS):
        g = []
        for q, (cx, cy, cz) in enumerate(Q):
            v = gn[x + cx + 1, q]
            d = x + cx + 2
            if cy == 1:
                v = jnp.where(last, rolly(gy[q], 127 - 8 - d), rolly(v, -1))
            if cy == -1:
                v = jnp.where(first, rolly(gy[q], -d), rolly(v, 1))
            g.append(rollz(v, -cz))
        got = pull_back(g, [uck[x, k] for k in range(3)], rates, wall_row(wall, x))
        for q in range(27):
            out[pl.ds(q * 32 + x, 8, stride=4), :] = got[q]


def shards(sizes, checkpoint, rates, wall_mask, cotangent):
    ck, cot = checkpoint.reshape(864, 128), cotangent.reshape(864, 128)
    wall, rates = wall_mask.reshape(32, 128), rates.reshape(1, 27)
    vmem, smem = pl.BlockSpec(memory_space=pltpu.VMEM), pl.BlockSpec(memory_space=pltpu.SMEM)
    small = dict(vmem_limit_bytes=16 << 20)

    def like(*shape):
        return jax.ShapeDtypeStruct(shape, F32)

    sxc, mb, ey, uck = pl.pallas_call(
        prepare,
        out_shape=(like(2, 27, 8, 128), like(6, 5, 8, 128), like(3, 2, 8, 128), like(4, 3, 8, 128)),
        in_specs=[vmem, vmem, vmem, smem],
        out_specs=(vmem,) * 4,
        compiler_params=pltpu.CompilerParams(**small),
        name="prepare",
    )(ck, cot, wall, rates)
    xc, xm, xe, en = pl.pallas_call(
        functools.partial(exchange, sizes),
        out_shape=(like(2, 27, 8, 128), like(2, 2, 5, 8, 128), like(2, 2, 8, 128), like(6, 3, 8, 128)),
        in_specs=[vmem] * 3,
        out_specs=(vmem,) * 4,
        scratch_shapes=[pltpu.SemaphoreType.DMA((12,)), pltpu.SemaphoreType.DMA((12,))],
        compiler_params=pltpu.CompilerParams(collective_id=0, has_side_effects=True, **small),
        name="exchange",
    )(sxc, mb, ey)
    grad = pl.pallas_call(
        finish,
        out_shape=like(864, 128),
        in_specs=[vmem, vmem, smem] + [vmem] * 7,
        out_specs=vmem,
        scratch_shapes=[pltpu.VMEM((6, 27, 8, 128), F32), pltpu.VMEM((27, 8, 128), F32)],
        compiler_params=pltpu.CompilerParams(**small),
        name="finish",
    )(cot, wall, rates, mb, ey, uck, xc, xm, xe, en)
    return grad.reshape(checkpoint.shape)


def solution(mesh):
    sizes = (mesh.shape["gx"], mesh.shape["gy"])
    in_specs = (P(None, None, "gx", "gy"), P(), P(None, "gx", "gy"), P(None, None, "gx", "gy"))
    out_specs = P(None, None, "gx", "gy")
    return jax.shard_map(
        functools.partial(shards, sizes), mesh=mesh, in_specs=in_specs, out_specs=out_specs, check_vma=False
    )
```

time: 85.9 us -> 26.4 us (0.31)
  the two profiles are of different devices: /device:TPU:25 before, /device:TPU:4 now
where the time goes in v1:
time: 26.4 us; the launch traced here: 26.1 us
  Pallas kernels  22.7 us (86%)
  local copies, waits for them, and re-layouts  3.4 us (13%)
    pallas_call x1, Pallas kernels, shards(): pl.pallas_call(functools.partial(exchange, sizes), out_shape=(like(2, 27,...  19.6 us
    unnamed x10, local copies, waits for them, and re-layouts  3.4 us
    pallas_call x1, Pallas kernels, shards(): pl.pallas_call(finish, out_shape=like(864, 128), in_specs=[vmem, vmem, sm...  2.11 us
    pallas_call x1, Pallas kernels, shards(): pl.pallas_call(prepare, out_shape=(like(2, 27, 8, 128), like(6, 5, 8, 128...  1.05 us

profile of v1, /device:TPU:4, one launch (start us, length us, event | category | flops | bytes accessed | tf_op | source)
XLA Modules:
  0.0 26.1 jit_solution(6472360737475156612)
XLA Ops:
  0.0 0.0 copy-start.4
  0.0 0.7 %copy-done.4 = f32[27]{0:T(128)S(1)} copy-done((f32[27]{0:T(128)S(1)}, f32[27]{0:T(128)}, u32[]{:S(2)}) %copy-start.4) | copy-done | bytes 132
  0.7 0.0 copy-start
  0.7 1.0 %copy-done = f32[27,8,4,128]{3,2,1,0:T(4,128)S(1)} copy-done((f32[27,8,4,128]{3,2,1,0:T(4,128)S(1)}, f32[27,8,4,128]{3,2,1,0:T(4,128)}, u32[]{:S(2)}) %copy-start) | copy-done | bytes 442392
  1.7 0.0 copy-start.2
  1.7 1.0 %copy-done.2 = f32[27,8,4,128]{3,2,1,0:T(4,128)S(1)} copy-done((f32[27,8,4,128]{3,2,1,0:T(4,128)S(1)}, f32[27,8,4,128]{3,2,1,0:T(4,128)}, u32[]{:S(2)}) %copy-start.2) | copy-done | bytes 442392
  2.7 0.0 copy-start.3
  2.7 0.7 %copy-done.3 = s32[8,4,128]{2,1,0:T(4,128)S(1)} copy-done((s32[8,4,128]{2,1,0:T(4,128)S(1)}, s32[8,4,128]{2,1,0:T(4,128)}, u32[]{:S(2)}) %copy-start.3) | copy-done | bytes 16408
  3.4 0.0 copy-start.1
  3.4 1.0 %prepare.1 = (f32[2,27,8,128]{3,2,1,0:T(8,128)S(1)}, f32[6,5,8,128]{3,2,1,0:T(8,128)S(1)}, f32[3,2,8,128]{3,2,1,0:T(8,128)S(1)}, f32[4,3,8,128]{3,2,1,0:T(8,128)S(1)}) custom-call(f32[864,128]{1,0:T(8,128)S(1)} %bitcast.7, f32[864,128]{1,0:T(8,128)S(1)} %bitcast.5, s32[32,128]{1,0:T(8,128)S(1)} %bitcast.8, f32[1,27]{1,0:T(1,128)S(1)} %bitcast.10), custom_call_target="tpu_custom_call" | custom-call | tf_op jit(solution)/shard_map/prepare/pallas_call | solution.py:380
  4.5 19.6 %exchange.1 = (f32[2,27,8,128]{3,2,1,0:T(8,128)S(1)}, f32[2,2,5,8,128]{4,3,2,1,0:T(8,128)S(1)}, f32[2,2,8,128]{3,2,1,0:T(8,128)S(1)}, f32[6,3,8,128]{3,2,1,0:T(8,128)S(1)}) custom-call(f32[2,27,8,128]{3,2,1,0:T(8,128)S(1)} %get-tuple-element.16.sxc, f32[6,5,8,128]{3,2,1,0:T(8,128)S(1)} %get-tuple-element.13.mb, f32[3,2,8,128]{3,2,1,0:T(8,128)S(1)} %get-tuple-element.14.ey), custom_call_target="tpu_custom_call" | custom-call | tf_op jit(solution)/shard_map/exchange/pallas_call | solution.py:388
  24.0 0.0 copy-done.1
  24.0 2.1 %finish.1 = f32[864,128]{1,0:T(8,128)} custom-call(f32[864,128]{1,0:T(8,128)S(1)} %bitcast.6, s32[32,128]{1,0:T(8,128)S(1)} %bitcast.9, f32[1,27]{1,0:T(1,128)S(1)} %bitcast.11, f32[6,5,8,128]{3,2,1,0:T(8,128)S(1)} %get-tuple-element.13.mb, f32[3,2,8,128]{3,2,1,0:T(8,128)S(1)} %get-tuple-element.14.ey, f32[4,3,8,128]{3,2,1,0:T(8,128)S(1)} %get-tuple-element.15.uck, ...), custom_call_target="tpu_custom_call" | custom-call | tf_op jit(solution)/shard_map/finish/pallas_call | solution.py:397
Async XLA Ops:
  0.0 0.7 %copy-start.4 = (f32[27]{0:T(128)S(1)}, f32[27]{0:T(128)}, u32[]{:S(2)}) copy-start(f32[27]{0:T(128)} %param.5) | copy-start | bytes 328
  0.7 1.0 %copy-start = (f32[27,8,4,128]{3,2,1,0:T(4,128)S(1)}, f32[27,8,4,128]{3,2,1,0:T(4,128)}, u32[]{:S(2)}) copy-start(f32[27,8,4,128]{3,2,1,0:T(4,128)} %param.7) | copy-start | bytes 1327108
  1.7 1.0 %copy-start.2 = (f32[27,8,4,128]{3,2,1,0:T(4,128)S(1)}, f32[27,8,4,128]{3,2,1,0:T(4,128)}, u32[]{:S(2)}) copy-start(f32[27,8,4,128]{3,2,1,0:T(4,128)} %param.4) | copy-start | bytes 1327108
  2.7 0.7 %copy-start.3 = (s32[8,4,128]{2,1,0:T(4,128)S(1)}, s32[8,4,128]{2,1,0:T(4,128)}, u32[]{:S(2)}) copy-start(s32[8,4,128]{2,1,0:T(4,128)} %param.6) | copy-start | bytes 49156
  3.4 20.6 %copy-start.1 = (f32[27,8,4,128]{3,2,1,0:T(4,128)S(1)}, f32[27,8,4,128]{3,2,1,0:T(4,128)}, u32[]{:S(2)}) copy-start(f32[27,8,4,128]{3,2,1,0:T(4,128)} %param.7) | copy-start | bytes 1327108

commit v2 on v1

--- a/solution.py
+++ b/solution.py
@@ -109,7 +109,7 @@
     e = g
     for axis in (2, 1, 0):
         e = along(e, axis, dual_doubled)
-    e = [e[n] * rates[n] for n in range(27)]
+    e = [e[n] * rates(n) for n in range(27)]
     e222 = e[at(2, 2, 2)] * NINTH
     pair_xy, pair_xz, pair_yz = e[at(2, 2, 0)], e[at(2, 0, 2)], e[at(0, 2, 2)]
     pxx = e[at(2, 0, 0)] + (pair_xy + pair_xz) * THIRD + e222
@@ -150,23 +150,112 @@
     return jnp.where((height == 0) | (height == 7), 1, mask).astype(F32)
 
 
-def prepare(ck, cot, wall, rates_ref, sxc, mb, ey, uck):
+def exchange(
+    sizes, ck_hbm, cot_hbm, wall_hbm, rates_hbm,
+    cot, mb, ey, uck, rv, xc, xm, xe, en,
+    ck, wall, rates_ref, sxc, ehi, load, ready, send, recv,
+):
+    nx, ny = sizes
     lane = lanes()
-    rates = halved_rates(rates_ref)
+
+    def device(dx, dy):
+        return (
+            lax.rem(lax.axis_index("gx") + (dx + nx), nx),
+            lax.rem(lax.axis_index("gy") + (dy + ny), ny),
+        )
+
+    def signal(sem, dx):
+        for dy in (0, 1, -1):
+            pl.semaphore_signal(sem, inc=1, device_id=device(dx, dy), device_id_type=MESH)
+
+    barrier = pltpu.get_barrier_semaphore()
+    signal(barrier, -1)
+    loads = []
+    for src, dst in ((cot_hbm, cot), (ck_hbm, ck), (wall_hbm, wall), (rates_hbm, rates_ref)):
+        loads.append(pltpu.make_async_copy(src, dst, load.at[len(loads)]))
+        loads[-1].start()
+    pl.semaphore_wait(barrier, 3)
+    signal(ready, 1)
+
+    copies = []
+
+    def put(src, dst, dx, dy):
+        n = len(copies)
+        copies.append(
+            pltpu.make_async_remote_copy(
+                src_ref=src,
+                dst_ref=dst,
+                send_sem=send.at[n],
+                recv_sem=recv.at[n],
+                device_id=device(dx, dy),
+                device_id_type=MESH,
+            )
+        )
+        copies[-1].start()
+
+    loads[0].wait()
     for q in range(18):
         sxc[1, q] = row(cot, q, 3)
+    for q in range(9):
+        sxc[1, 18 + q] = row(cot, q, 2)
+    put(sxc.at[1], xc.at[0], 1, 0)
+    for q in range(18):
         sxc[0, q] = row(cot, q + 9, 0)
     for q in range(9):
-        sxc[1, 18 + q] = row(cot, q, 2)
         sxc[0, 18 + q] = row(cot, q + 18, 1)
 
     zero = jnp.zeros((8, 128), F32)
     first, last = lane == 0, lane == 127
     body = [[zero] * 4 for _ in range(6)]
     edge = [[zero] * 3 for _ in range(6)]
-    for x in range(ROWS):
+    acc = dict.fromkeys(("r0", "r1", "r2", "l0", "l1", "l2", "l0m"), zero)
+
+    def add(name, v, d):
+        acc[name] = jnp.where(lane == d, v, acc[name])
+
+    def pack_cotangent(x):
+        for i, (cx, cz) in enumerate([(a, c) for a in range(3) for c in range(3)]):
+            d = 8 * i + x + 2
+            v = rolly(row(cot, at(cx, 0, cz), x), d - 127)
+            add("r0", v, d)
+            add("r2", v, d - 1)
+            v = rolly(row(cot, at(cx, 2, cz), x), d)
+            add("l0", v, d)
+            add("l2", v, d + 1)
+            v = rolly(row(cot, at(cx, 1, cz), x), d - 127)
+            add("r1", v, d)
+            add("l1", v, d + 1)
+
+    def pack_sums(r):
+        outer = edge[r]
+        outer = [outer[0], outer[1], jnp.where(first, outer[0], -outer[0]), outer[2]]
+        for k in range(4):
+            d = 8 * (9 + k) + r + 1
+            v = rolly(body[r][k], d - 127)
+            add("r1", v, d)
+            add("l1", v, d + 1)
+            v = rolly(outer[k], d)
+            add("r0", v, d)
+            add("l0m", v, d - 1)
+
+    def pack_wall(x, w):
+        d = 8 * 13 + x + 2
+        v = rolly(w, d - 127)
+        add("r1", v, d)
+        add("l1", v, d + 1)
+
+    def store_packs(ref):
+        ref[0, 0] = acc["l0"] + rolly(acc["l0m"], 1)
+        ref[1, 0] = rolly(acc["l1"], -1)
+        ref[2, 0] = rolly(acc["l2"], -1)
+        ref[0, 1] = acc["r0"]
+        ref[1, 1] = acc["r1"]
+        ref[2, 1] = rolly(acc["r2"], 1)
+
+    def collide_row(x):
         w = wall_row(wall, x)
         mb[x + 1, 4] = w
+        pack_wall(x, w)
         out, u = collide([row(ck, q, x) for q in range(27)], rates, w)
         for k in range(3):
             uck[x, k] = u[k]
@@ -192,96 +281,58 @@
                 body[r][1] = body[r][1] + (a - 1) * total
             body[r][2] = body[r][2] + (ap - am)
             body[r][3] = body[r][3] + (tilts[1] + (bp + bm))
-    for r in range(6):
+
+    def store_sums(r):
         for k in range(4):
             mb[r, k] = body[r][k]
+        pack_sums(r)
+
+    pack_cotangent(3)
+    pack_cotangent(2)
+    for c in loads[1:]:
+        c.wait()
+    rates = halved_rates(rates_ref)
+    mb[5, 4] = zero
+    collide_row(3)
+    collide_row(2)
+    store_sums(5)
+    store_sums(4)
+    store_packs(ehi)
+    put(ehi.at[:, 1], en.at[1], 1, 1)
+    put(ehi.at[:, 0], en.at[4], 1, -1)
+    put(mb.at[pl.ds(4, 2)], xm.at[0], 1, 0)
+    put(ehi.at[0], xe.at[0], 1, 0)
+
     mb[0, 4] = zero
-    mb[5, 4] = zero
-
-    r0, r1, r2, l0, l1, l2, l0m = [zero] * 7
-    for i, (cx, cz) in enumerate([(a, c) for a in range(3) for c in range(3)]):
-        for x in range(ROWS):
-            d = 8 * i + x + 2
-            here, before, after = lane == d, lane == d - 1, lane == d + 1
-            v = rolly(row(cot, at(cx, 0, cz), x), d - 127)
-            r0, r2 = jnp.where(here, v, r0), jnp.where(before, v, r2)
-            v = rolly(row(cot, at(cx, 2, cz), x), d)
-            l0, l2 = jnp.where(here, v, l0), jnp.where(after, v, l2)
-            v = rolly(row(cot, at(cx, 1, cz), x), d - 127)
-            r1, l1 = jnp.where(here, v, r1), jnp.where(after, v, l1)
-    for r in range(6):
-        outer = edge[r]
-        outer = [outer[0], outer[1], jnp.where(first, outer[0], -outer[0]), outer[2]]
-        for k in range(4):
-            d = 8 * (9 + k) + r + 1
-            here, before, after = lane == d, lane == d - 1, lane == d + 1
-            v = rolly(body[r][k], d - 127)
-            r1, l1 = jnp.where(here, v, r1), jnp.where(after, v, l1)
-            v = rolly(outer[k], d)
-            r0, l0m = jnp.where(here, v, r0), jnp.where(before, v, l0m)
-    for x in range(ROWS):
-        d = 8 * 13 + x + 2
-        v = rolly(wall_row(wall, x), d - 127)
-        r1, l1 = jnp.where(lane == d, v, r1), jnp.where(lane == d + 1, v, l1)
-    ey[0, 0] = l0 + rolly(l0m, 1)
-    ey[1, 0] = rolly(l1, -1)
-    ey[2, 0] = rolly(l2, -1)
-    ey[0, 1] = r0
-    ey[1, 1] = r1
-    ey[2, 1] = rolly(r2, 1)
-
-
-def exchange(sizes, sxc, mb, ey, xc, xm, xe, en, send, recv):
-    nx, ny = sizes
-
-    def device(dx, dy):
-        return (
-            lax.rem(lax.axis_index("gx") + (dx + nx), nx),
-            lax.rem(lax.axis_index("gy") + (dy + ny), ny),
-        )
-
-    around = [(a, b) for a in (1, 0, -1) for b in (1, 0, -1) if (a, b) != (0, 0)]
-    barrier = pltpu.get_barrier_semaphore()
-    for d in around:
-        pl.semaphore_signal(barrier, inc=1, device_id=device(*d), device_id_type=MESH)
-    pl.semaphore_wait(barrier, 8)
-    copies = []
-
-    def put(src, dst, dx, dy):
-        n = len(copies)
-        copies.append(
-            pltpu.make_async_remote_copy(
-                src_ref=src,
-                dst_ref=dst,
-                send_sem=send.at[n],
-                recv_sem=recv.at[n],
-                device_id=device(dx, dy),
-                device_id_type=MESH,
-            )
-        )
-        copies[-1].start()
-
-    put(ey.at[:, 1], en.at[1], 1, 1)
-    put(ey.at[:, 0], en.at[4], 1, -1)
-    put(mb.at[pl.ds(4, 2)], xm.at[0], 1, 0)
-    put(ey.at[0], xe.at[0], 1, 0)
-    put(sxc.at[1], xc.at[0], 1, 0)
+    pack_cotangent(1)
+    pack_cotangent(0)
+    collide_row(1)
+    collide_row(0)
+    for r in range(4):
+        store_sums(r)
+    store_packs(ey)
+    pl.semaphore_wait(ready, 3)
+    put(sxc.at[0], xc.at[1], -1, 0)
     put(ey.at[:, 1], en.at[2], -1, 1)
     put(ey.at[:, 0], en.at[5], -1, -1)
     put(mb.at[pl.ds(0, 2)], xm.at[1], -1, 0)
     put(ey.at[0], xe.at[1], -1, 0)
-    put(sxc.at[0], xc.at[1], -1, 0)
     put(ey.at[:, 1], en.at[0], 0, 1)
     put(ey.at[:, 0], en.at[3], 0, -1)
+    for n in range(27):
+        rv[n] = jnp.full((8, 128), rates[n], F32)
     for c in copies:
         c.wait_recv()
     for c in copies:
         c.wait_send()
 
 
-def finish(cot, wall, rates_ref, mb, ey, uck, xc, xm, xe, en, out, gn, gy):
+def finish(cot, mb, ey, uck, rv, xc, xm, xe, en, out, gn, gy):
     lane = lanes()
-    rates = halved_rates(rates_ref)
+
+    def rates(n):
+        return rv[n]
+
     first, last = lane == 0, lane == 127
     low, high = lane % 8 < 3, lane % 8 >= 5
     left = lane < 8
@@ -337,7 +388,7 @@
             v = v + jnp.where(first, rolly(exl[0], -d), 0.0)
             v = v + jnp.where(last, rolly(exr[0], 127 - d), 0.0)
             m.append(v)
-        w = xm[0, 0, 4] if x < 0 else xm[1, 1, 4] if x == ROWS else wall_row(wall, x)
+        w = xm[0, 0, 4] if x < 0 else xm[1, 1, 4] if x == ROWS else mb[x + 1, 4]
         g = []
         for q, (cx, cy, cz) in enumerate(Q):
             v = source(q, x + cx)
@@ -363,7 +414,7 @@
             if cy == -1:
                 v = jnp.where(first, rolly(gy[q], -d), rolly(v, 1))
             g.append(rollz(v, -cz))
-        got = pull_back(g, [uck[x, k] for k in range(3)], rates, wall_row(wall, x))
+        got = pull_back(g, [uck[x, k] for k in range(3)], rates, mb[x + 1, 4])
         for q in range(27):
             out[pl.ds(q * 32 + x, 8, stride=4), :] = got[q]
 
@@ -371,38 +422,43 @@
 def shards(sizes, checkpoint, rates, wall_mask, cotangent):
     ck, cot = checkpoint.reshape(864, 128), cotangent.reshape(864, 128)
     wall, rates = wall_mask.reshape(32, 128), rates.reshape(1, 27)
-    vmem, smem = pl.BlockSpec(memory_space=pltpu.VMEM), pl.BlockSpec(memory_space=pltpu.SMEM)
+    vmem, hbm = pl.BlockSpec(memory_space=pltpu.VMEM), pl.BlockSpec(memory_space=pltpu.HBM)
     small = dict(vmem_limit_bytes=16 << 20)
 
     def like(*shape):
         return jax.ShapeDtypeStruct(shape, F32)
 
-    sxc, mb, ey, uck = pl.pallas_call(
-        prepare,
-        out_shape=(like(2, 27, 8, 128), like(6, 5, 8, 128), like(3, 2, 8, 128), like(4, 3, 8, 128)),
-        in_specs=[vmem, vmem, vmem, smem],
-        out_specs=(vmem,) * 4,
-        compiler_params=pltpu.CompilerParams(**small),
-        name="prepare",
-    )(ck, cot, wall, rates)
-    xc, xm, xe, en = pl.pallas_call(
+    got = pl.pallas_call(
         functools.partial(exchange, sizes),
-        out_shape=(like(2, 27, 8, 128), like(2, 2, 5, 8, 128), like(2, 2, 8, 128), like(6, 3, 8, 128)),
-        in_specs=[vmem] * 3,
-        out_specs=(vmem,) * 4,
-        scratch_shapes=[pltpu.SemaphoreType.DMA((12,)), pltpu.SemaphoreType.DMA((12,))],
+        out_shape=(
+            like(864, 128), like(6, 5, 8, 128), like(3, 2, 8, 128), like(4, 3, 8, 128), like(27, 8, 128),
+            like(2, 27, 8, 128), like(2, 2, 5, 8, 128), like(2, 2, 8, 128), like(6, 3, 8, 128),
+        ),
+        in_specs=[hbm] * 4,
+        out_specs=(vmem,) * 9,
+        scratch_shapes=[
+            pltpu.VMEM((864, 128), F32),
+            pltpu.VMEM((32, 128), jnp.int32),
+            pltpu.SMEM((1, 27), F32),
+            pltpu.VMEM((2, 27, 8, 128), F32),
+            pltpu.VMEM((3, 2, 8, 128), F32),
+            pltpu.SemaphoreType.DMA((4,)),
+            pltpu.SemaphoreType.REGULAR,
+            pltpu.SemaphoreType.DMA((12,)),
+            pltpu.SemaphoreType.DMA((12,)),
+        ],
         compiler_params=pltpu.CompilerParams(collective_id=0, has_side_effects=True, **small),
         name="exchange",
-    )(sxc, mb, ey)
+    )(*[pltpu.with_memory_space_constraint(v, pltpu.HBM) for v in (ck, cot, wall, rates)])
     grad = pl.pallas_call(
         finish,
         out_shape=like(864, 128),
-        in_specs=[vmem, vmem, smem] + [vmem] * 7,
+        in_specs=[vmem] * 9,
         out_specs=vmem,
         scratch_shapes=[pltpu.VMEM((6, 27, 8, 128), F32), pltpu.VMEM((27, 8, 128), F32)],
         compiler_params=pltpu.CompilerParams(**small),
         name="finish",
-    )(cot, wall, rates, mb, ey, uck, xc, xm, xe, en)
+    )(*got)
     return grad.reshape(checkpoint.shape)
 
 

time: 26.4 us -> 21.6 us (0.82)
  the two profiles are of different devices: /device:TPU:4 before, /device:TPU:1 now
where the time goes in v2:
time: 21.6 us; the launch traced here: 21.5 us
  Pallas kernels  21.5 us (100%)
    pallas_call x1, Pallas kernels, shards(): pl.pallas_call(functools.partial(exchange, sizes), out_shape=(like(864, 1...  19.9 us
    pallas_call x1, Pallas kernels, shards(): pl.pallas_call(finish, out_shape=like(864, 128), in_specs=[vmem] * 9, out...  1.57 us

profile of v2, /device:TPU:1, one launch (start us, length us, event | category | flops | bytes accessed | tf_op | source)
XLA Modules:
  0.0 21.5 jit_solution(8071895053234635801)
XLA Ops:
  0.0 19.9 %exchange.1 = (f32[864,128]{1,0:T(8,128)S(1)}, f32[6,5,8,128]{3,2,1,0:T(8,128)S(1)}, f32[3,2,8,128]{3,2,1,0:T(8,128)S(1)}, f32[4,3,8,128]{3,2,1,0:T(8,128)S(1)},...) custom-call(f32[864,128]{1,0:T(8,128)} %bitcast.5, ...), custom_call_target="tpu_custom_call" | custom-call | tf_op jit(solution)/shard_map/exchange/pallas_call | solution.py:431
  19.9 1.6 %finish.1 = f32[864,128]{1,0:T(8,128)} custom-call(f32[864,128]{1,0:T(8,128)S(1)} %get-tuple-element.14.cot, f32[6,5,8,128]{3,2,1,0:T(8,128)S(1)} %get-tuple-element.15.mb, f32[3,2,8,128]{3,2,1,0:T(8,128)S(1)} %get-tuple-element.16.ey, f32[4,3,8,128]{3,2,1,0:T(8,128)S(1)} %get-tuple-element.17.uck, f32[27,8,128]{2,1,0:T(8,128)S(1)} %get-tuple-element.18.rv, ...), custom_call_target="tpu_custom_call" | custom-call | tf_op jit(solution)/shard_map/finish/pallas_call | solution.py:453

commit v3 on v2

--- a/solution.py
+++ b/solution.py
@@ -150,10 +150,111 @@
     return jnp.where((height == 0) | (height == 7), 1, mask).astype(F32)
 
 
+def merged(en, ey, xe, below):
+    lane = lanes()
+    low, high = lane % 8 < 3, lane % 8 >= 5
+
+    def merge(own, lower, upper):
+        own = own + jnp.where(high, rolly(upper, 4), 0.0)
+        return own + jnp.where(low, rolly(lower, -4), 0.0) if below else own
+
+    exl = [merge(en[0, k], en[1, k], en[2, k]) for k in range(3)]
+    exr = [merge(en[3, k], en[4, k], en[5, k]) for k in range(3)]
+    oxl = merge(ey[0, 0], xe[0, 0], xe[1, 0])
+    oxr = merge(ey[0, 1], xe[0, 1], xe[1, 1])
+    return exl, exr, oxl, oxr
+
+
+def slot(q):
+    return 3 * (q // 9) + q % 3
+
+
+def pull_beside(packs, rates, gy):
+    exl, exr, oxl, oxr = packs
+    lane = lanes()
+    left = lane < 8
+    g = []
+    for q, (cx, cy, cz) in enumerate(Q):
+        s = slot(q)
+        lo, hi = ((exl[2], oxr), (exl[1], exr[1]), (oxl, exr[2]))[cy + 1]
+        v = jnp.where(left, rolly(lo, -8 * s - cx), rolly(hi, 8 - 8 * s - cx))
+        g.append(rollz(v, -cz))
+    m = []
+    lo, hi = exl[1] + oxl, exr[1] + oxr
+    for k in range(4):
+        s = 9 + k
+        m.append(jnp.where(left, rolly(lo, -8 * s), rolly(hi, 8 - 8 * s)))
+    w = jnp.where(left, rolly(exl[1], -104), rolly(exr[1], -96))
+    inv = 1.0 / jnp.where(m[0] > 0.0, m[0], 1.0)
+    got = pull_back(g, [m[k] * inv for k in (1, 2, 3)], rates, w)
+    for q, (cx, cy, cz) in enumerate(Q):
+        if cy != 0:
+            gy[q] = got[q]
+
+
+def pull_row(x, packs, rates, cot, mb, xc, xm, gn):
+    exl, exr = packs[0][0], packs[1][0]
+    lane = lanes()
+    first, last = lane == 0, lane == 127
+
+    def source(q, x):
+        if 0 <= x < ROWS:
+            return row(cot, q, x)
+        if x == -1:
+            return xc[0, q]
+        if x == -2:
+            return xc[0, 18 + q]
+        return xc[1, q - 9] if x == ROWS else xc[1, q]
+
+    m = []
+    for k in range(4):
+        v = mb[x + 1, k]
+        if x <= 0:
+            v = v + xm[0, x + 1, k]
+        if x >= 3:
+            v = v + xm[1, x - 3, k]
+        d = 8 * (9 + k) + x + 2
+        v = v + jnp.where(first, rolly(exl, -d), 0.0)
+        v = v + jnp.where(last, rolly(exr, 127 - d), 0.0)
+        m.append(v)
+    w = xm[0, 0, 4] if x < 0 else xm[1, 1, 4] if x == ROWS else mb[x + 1, 4]
+    g = []
+    for q, (cx, cy, cz) in enumerate(Q):
+        v = source(q, x + cx)
+        d = 8 * slot(q) + x + cx + 2
+        if cy == 1:
+            v = jnp.where(last, rolly(exr, 127 - d), rolly(v, -1))
+        if cy == -1:
+            v = jnp.where(first, rolly(exl, -d), rolly(v, 1))
+        g.append(rollz(v, -cz))
+    inv = 1.0 / m[0]
+    keep = range(9) if x < 0 else range(18, 27) if x == ROWS else range(27)
+    got = pull_back(g, [m[k] * inv for k in (1, 2, 3)], rates, w, keep)
+    for q in keep:
+        gn[q] = got[q]
+
+
+def pull_first(x, rates, uck, mb, gn, gy, out):
+    lane = lanes()
+    first, last = lane == 0, lane == 127
+    g = []
+    for q, (cx, cy, cz) in enumerate(Q):
+        v = gn(x + cx)[q]
+        d = x + cx + 2
+        if cy == 1:
+            v = jnp.where(last, rolly(gy[q], 127 - 8 - d), rolly(v, -1))
+        if cy == -1:
+            v = jnp.where(first, rolly(gy[q], -d), rolly(v, 1))
+        g.append(rollz(v, -cz))
+    got = pull_back(g, [uck[x, k] for k in range(3)], rates, mb[x + 1, 4])
+    for q in range(27):
+        out[q] = got[q]
+
+
 def exchange(
     sizes, ck_hbm, cot_hbm, wall_hbm, rates_hbm,
-    cot, mb, ey, uck, rv, xc, xm, xe, en,
-    ck, wall, rates_ref, sxc, ehi, load, ready, send, recv,
+    cot, mb, ey, uck, rv, xc, xm, xe, en, upper, done,
+    ck, wall, rates_ref, ehi, gy, load, ready, send, recv,
 ):
     nx, ny = sizes
     lane = lanes()
@@ -171,13 +272,12 @@
     barrier = pltpu.get_barrier_semaphore()
     signal(barrier, -1)
     loads = []
-    for src, dst in ((cot_hbm, cot), (ck_hbm, ck), (wall_hbm, wall), (rates_hbm, rates_ref)):
+    for src, dst in ((cot_hbm.reshape(864, 128), cot), (ck_hbm, ck), (wall_hbm, wall), (rates_hbm, rates_ref)):
         loads.append(pltpu.make_async_copy(src, dst, load.at[len(loads)]))
         loads[-1].start()
     pl.semaphore_wait(barrier, 3)
-    signal(ready, 1)
-
-    copies = []
+
+    copies, late, soon = [], [], []
 
     def put(src, dst, dx, dy):
         n = len(copies)
@@ -192,17 +292,12 @@
             )
         )
         copies[-1].start()
-
+        (late if dx == 1 else soon).append(copies[-1])
+
+    put(cot_hbm.at[pl.ds(0, 18), :, 3], xc.at[0, pl.ds(0, 18)], 1, 0)
+    put(cot_hbm.at[pl.ds(0, 9), :, 2], xc.at[0, pl.ds(18, 9)], 1, 0)
+    signal(ready, 1)
     loads[0].wait()
-    for q in range(18):
-        sxc[1, q] = row(cot, q, 3)
-    for q in range(9):
-        sxc[1, 18 + q] = row(cot, q, 2)
-    put(sxc.at[1], xc.at[0], 1, 0)
-    for q in range(18):
-        sxc[0, q] = row(cot, q + 9, 0)
-    for q in range(9):
-        sxc[0, 18 + q] = row(cot, q + 18, 1)
 
     zero = jnp.zeros((8, 128), F32)
     first, last = lane == 0, lane == 127
@@ -312,7 +407,8 @@
         store_sums(r)
     store_packs(ey)
     pl.semaphore_wait(ready, 3)
-    put(sxc.at[0], xc.at[1], -1, 0)
+    put(cot_hbm.at[pl.ds(9, 18), :, 0], xc.at[1, pl.ds(0, 18)], -1, 0)
+    put(cot_hbm.at[pl.ds(18, 9), :, 1], xc.at[1, pl.ds(18, 9)], -1, 0)
     put(ey.at[:, 1], en.at[2], -1, 1)
     put(ey.at[:, 0], en.at[5], -1, -1)
     put(mb.at[pl.ds(0, 2)], xm.at[1], -1, 0)
@@ -321,106 +417,54 @@
     put(ey.at[:, 0], en.at[3], 0, -1)
     for n in range(27):
         rv[n] = jnp.full((8, 128), rates[n], F32)
-    for c in copies:
+
+    for c in soon:
+        c.wait_recv()
+
+    def known(n):
+        return rv[n]
+
+    packs = merged(en, ey, xe, False)
+    for x in (4, 3, 2, 1):
+        pull_row(x, packs, known, cot, mb, xc, xm, upper.at[x - 1])
+    pull_beside(packs, known, gy)
+    for x in (3, 2):
+        pull_first(x, known, uck, mb, lambda x: upper.at[x - 1], gy, done.at[x - 2])
+    for c in late:
         c.wait_recv()
     for c in copies:
         c.wait_send()
 
 
-def finish(cot, mb, ey, uck, rv, xc, xm, xe, en, out, gn, gy):
-    lane = lanes()
-
+def finish(cot, mb, ey, uck, rv, xc, xm, xe, en, upper, done, out, lower, gy, ends, sems):
     def rates(n):
         return rv[n]
 
-    first, last = lane == 0, lane == 127
-    low, high = lane % 8 < 3, lane % 8 >= 5
-    left = lane < 8
-
-    def merge(own, below, above):
-        below, above = rolly(below, -4), rolly(above, 4)
-        return own + jnp.where(low, below, 0.0) + jnp.where(high, above, 0.0)
-
-    exl = [merge(en[0, k], en[1, k], en[2, k]) for k in range(3)]
-    exr = [merge(en[3, k], en[4, k], en[5, k]) for k in range(3)]
-    oxl = merge(ey[0, 0], xe[0, 0], xe[1, 0])
-    oxr = merge(ey[0, 1], xe[0, 1], xe[1, 1])
-
-    def source(q, x):
-        if 0 <= x < ROWS:
-            return row(cot, q, x)
-        if x == -1:
-            return xc[0, q]
-        if x == -2:
-            return xc[0, 18 + q]
-        return xc[1, q - 9] if x == ROWS else xc[1, q]
-
-    def slot(q):
-        return 3 * (q // 9) + q % 3
-
-    g = []
-    for q, (cx, cy, cz) in enumerate(Q):
-        s = slot(q)
-        lo, hi = ((exl[2], oxr), (exl[1], exr[1]), (oxl, exr[2]))[cy + 1]
-        v = jnp.where(left, rolly(lo, -8 * s - cx), rolly(hi, 8 - 8 * s - cx))
-        g.append(rollz(v, -cz))
-    m = []
-    for k in range(4):
-        s = 9 + k
-        lo, hi = exl[1] + oxl, exr[1] + oxr
-        m.append(jnp.where(left, rolly(lo, -8 * s), rolly(hi, 8 - 8 * s)))
-    w = jnp.where(left, rolly(exl[1], -104), rolly(exr[1], -96))
-    inv = 1.0 / jnp.where((lane < 16) & (lane % 8 > 0) & (lane % 8 < 7), m[0], 1.0)
-    got = pull_back(g, [m[k] * inv for k in (1, 2, 3)], rates, w)
-    for q, (cx, cy, cz) in enumerate(Q):
-        if cy != 0:
-            gy[q] = got[q]
-
-    for x in range(-1, ROWS + 1):
-        m = []
-        for k in range(4):
-            v = mb[x + 1, k]
-            if x <= 0:
-                v = v + xm[0, x + 1, k]
-            if x >= 3:
-                v = v + xm[1, x - 3, k]
-            d = 8 * (9 + k) + x + 2
-            v = v + jnp.where(first, rolly(exl[0], -d), 0.0)
-            v = v + jnp.where(last, rolly(exr[0], 127 - d), 0.0)
-            m.append(v)
-        w = xm[0, 0, 4] if x < 0 else xm[1, 1, 4] if x == ROWS else mb[x + 1, 4]
-        g = []
-        for q, (cx, cy, cz) in enumerate(Q):
-            v = source(q, x + cx)
-            d = 8 * slot(q) + x + cx + 2
-            if cy == 1:
-                v = jnp.where(last, rolly(exr[0], 127 - d), rolly(v, -1))
-            if cy == -1:
-                v = jnp.where(first, rolly(exl[0], -d), rolly(v, 1))
-            g.append(rollz(v, -cz))
-        inv = 1.0 / m[0]
-        keep = range(9) if x < 0 else range(18, 27) if x == ROWS else range(27)
-        got = pull_back(g, [m[k] * inv for k in (1, 2, 3)], rates, w, keep)
-        for q in keep:
-            gn[x + 1, q] = got[q]
-
-    for x in range(ROWS):
-        g = []
-        for q, (cx, cy, cz) in enumerate(Q):
-            v = gn[x + cx + 1, q]
-            d = x + cx + 2
-            if cy == 1:
-                v = jnp.where(last, rolly(gy[q], 127 - 8 - d), rolly(v, -1))
-            if cy == -1:
-                v = jnp.where(first, rolly(gy[q], -d), rolly(v, 1))
-            g.append(rollz(v, -cz))
-        got = pull_back(g, [uck[x, k] for k in range(3)], rates, mb[x + 1, 4])
-        for q in range(27):
-            out[pl.ds(q * 32 + x, 8, stride=4), :] = got[q]
+    def gn(x):
+        return lower.at[x + 1] if x <= 0 else upper.at[x - 1]
+
+    copies = []
+
+    def put(src, x):
+        copies.append(pltpu.make_async_copy(src, out.at[:, :, x], sems.at[x]))
+        copies[-1].start()
+
+    put(done.at[0], 2)
+    put(done.at[1], 3)
+    packs = merged(en, ey, xe, True)
+    pull_beside(packs, rates, gy)
+    pull_row(0, packs, rates, cot, mb, xc, xm, gn(0))
+    pull_first(1, rates, uck, mb, gn, gy, ends.at[1])
+    put(ends.at[1], 1)
+    pull_row(-1, packs, rates, cot, mb, xc, xm, gn(-1))
+    pull_first(0, rates, uck, mb, gn, gy, ends.at[0])
+    put(ends.at[0], 0)
+    for c in copies:
+        c.wait()
 
 
 def shards(sizes, checkpoint, rates, wall_mask, cotangent):
-    ck, cot = checkpoint.reshape(864, 128), cotangent.reshape(864, 128)
+    ck = checkpoint.reshape(864, 128)
     wall, rates = wall_mask.reshape(32, 128), rates.reshape(1, 27)
     vmem, hbm = pl.BlockSpec(memory_space=pltpu.VMEM), pl.BlockSpec(memory_space=pltpu.HBM)
     small = dict(vmem_limit_bytes=16 << 20)
@@ -433,33 +477,38 @@
         out_shape=(
             like(864, 128), like(6, 5, 8, 128), like(3, 2, 8, 128), like(4, 3, 8, 128), like(27, 8, 128),
             like(2, 27, 8, 128), like(2, 2, 5, 8, 128), like(2, 2, 8, 128), like(6, 3, 8, 128),
+            like(4, 27, 8, 128), like(2, 27, 8, 128),
         ),
         in_specs=[hbm] * 4,
-        out_specs=(vmem,) * 9,
+        out_specs=(vmem,) * 11,
         scratch_shapes=[
             pltpu.VMEM((864, 128), F32),
             pltpu.VMEM((32, 128), jnp.int32),
             pltpu.SMEM((1, 27), F32),
-            pltpu.VMEM((2, 27, 8, 128), F32),
             pltpu.VMEM((3, 2, 8, 128), F32),
+            pltpu.VMEM((27, 8, 128), F32),
             pltpu.SemaphoreType.DMA((4,)),
             pltpu.SemaphoreType.REGULAR,
-            pltpu.SemaphoreType.DMA((12,)),
-            pltpu.SemaphoreType.DMA((12,)),
+            pltpu.SemaphoreType.DMA((14,)),
+            pltpu.SemaphoreType.DMA((14,)),
         ],
         compiler_params=pltpu.CompilerParams(collective_id=0, has_side_effects=True, **small),
         name="exchange",
-    )(*[pltpu.with_memory_space_constraint(v, pltpu.HBM) for v in (ck, cot, wall, rates)])
-    grad = pl.pallas_call(
+    )(*[pltpu.with_memory_space_constraint(v, pltpu.HBM) for v in (ck, cotangent, wall, rates)])
+    return pl.pallas_call(
         finish,
-        out_shape=like(864, 128),
-        in_specs=[vmem] * 9,
-        out_specs=vmem,
-        scratch_shapes=[pltpu.VMEM((6, 27, 8, 128), F32), pltpu.VMEM((27, 8, 128), F32)],
+        out_shape=like(27, 8, 4, 128),
+        in_specs=[vmem] * 11,
+        out_specs=hbm,
+        scratch_shapes=[
+            pltpu.VMEM((2, 27, 8, 128), F32),
+            pltpu.VMEM((27, 8, 128), F32),
+            pltpu.VMEM((2, 27, 8, 128), F32),
+            pltpu.SemaphoreType.DMA((4,)),
+        ],
         compiler_params=pltpu.CompilerParams(**small),
         name="finish",
     )(*got)
-    return grad.reshape(checkpoint.shape)
 
 
 def solution(mesh):

time: 21.6 us -> 20.5 us (0.949)
  Pallas kernels: 21.5 us -> 20.4 us
    pallas_call x1, Pallas kernels: 19.9 us -> 19.2 us  [shards(): pl.pallas_call(functools.partial(exchange, sizes), out_shape=(like(864, 1...]
    pallas_call x1, Pallas kernels: 1.57 us -> 1.18 us  [shards(): pl.pallas_call(finish, out_shape=like(27, 8, 4, 128), in_specs=[vmem] * 1...]
where the time goes in v3:
time: 20.5 us; the launch traced here: 20.4 us
  Pallas kernels  20.4 us (100%)
    pallas_call x1, Pallas kernels, shards(): pl.pallas_call(functools.partial(exchange, sizes), out_shape=(like(864, 1...  19.2 us
    pallas_call x1, Pallas kernels, shards(): pl.pallas_call(finish, out_shape=like(27, 8, 4, 128), in_specs=[vmem] * 1...  1.18 us

profile of v3, /device:TPU:1, one launch (start us, length us, event | category | flops | bytes accessed | tf_op | source)
XLA Modules:
  0.0 20.4 jit_solution(6744712850449594437)
XLA Ops:
  0.0 19.2 %exchange.1 = (f32[864,128]{1,0:T(8,128)S(1)}, f32[6,5,8,128]{3,2,1,0:T(8,128)S(1)}, f32[3,2,8,128]{3,2,1,0:T(8,128)S(1)}, f32[4,3,8,128]{3,2,1,0:T(8,128)S(1)},...) custom-call(f32[864,128]{1,0:T(8,128)} %bitcast.3, ...), custom_call_target="tpu_custom_call" | custom-call | tf_op jit(solution)/shard_map/exchange/pallas_call | solution.py:475
  19.2 1.2 %finish.1 = f32[27,8,4,128]{3,2,1,0:T(4,128)} custom-call(f32[864,128]{1,0:T(8,128)S(1)} %get-tuple-element.16.cot, f32[6,5,8,128]{3,2,1,0:T(8,128)S(1)} %get-tuple-element.17.mb, f32[3,2,8,128]{3,2,1,0:T(8,128)S(1)} %get-tuple-element.18.ey, f32[4,3,8,128]{3,2,1,0:T(8,128)S(1)} %get-tuple-element.19.uck, f32[27,8,128]{2,1,0:T(8,128)S(1)} %get-tuple-element.20.rv, ...), custom_call_target="tpu_custom_call" | custom-call | tf_op jit(solution)/shard_map/finish/pallas_call | solution.py:498

commit v4 on v3

--- a/solution.py
+++ b/solution.py
@@ -150,19 +150,29 @@
     return jnp.where((height == 0) | (height == 7), 1, mask).astype(F32)
 
 
-def merged(en, ey, xe, below):
-    lane = lanes()
-    low, high = lane % 8 < 3, lane % 8 >= 5
-
-    def merge(own, lower, upper):
-        own = own + jnp.where(high, rolly(upper, 4), 0.0)
-        return own + jnp.where(low, rolly(lower, -4), 0.0) if below else own
-
-    exl = [merge(en[0, k], en[1, k], en[2, k]) for k in range(3)]
-    exr = [merge(en[3, k], en[4, k], en[5, k]) for k in range(3)]
-    oxl = merge(ey[0, 0], xe[0, 0], xe[1, 0])
-    oxr = merge(ey[0, 1], xe[0, 1], xe[1, 1])
+def merged(en, ep, ey, below):
+    lane = lanes() % 8
+
+    def ends(v, k, low):
+        if low:
+            return jnp.where(lane < (2 if k == 2 else 3), rolly(v, (-4, -1, -7)[k]), 0.0)
+        return jnp.where(lane >= (6 if k == 2 else 5), rolly(v, (4, 1, -1)[k]), 0.0)
+
+    def merge(own, k, which):
+        own = own + ends(ep[3 + which], k, False)
+        return own + ends(ep[which], k, True) if below else own
+
+    exl = [merge(en[0, k], k, 0) for k in range(3)]
+    exr = [merge(en[1, k], k, 1) for k in range(3)]
+    oxl = merge(ey[0, 0], 0, 2)
+    oxr = merge(ey[0, 1], 1, 2)
     return exl, exr, oxl, oxr
+
+
+def field(r, k):
+    if r == 0:
+        return {0: 2, 2: 3, 3: 4, 1: 0, 4: 1}[k]
+    return 5 * r + {0: 0, 2: 1, 3: 2, 1: 3, 4: 4}[k]
 
 
 def slot(q):
@@ -192,8 +202,7 @@
             gy[q] = got[q]
 
 
-def pull_row(x, packs, rates, cot, mb, xc, xm, gn):
-    exl, exr = packs[0][0], packs[1][0]
+def pull_row(x, exl, exr, rates, cot, mb, xc, xm, gn):
     lane = lanes()
     first, last = lane == 0, lane == 127
 
@@ -208,16 +217,20 @@
 
     m = []
     for k in range(4):
-        v = mb[x + 1, k]
-        if x <= 0:
-            v = v + xm[0, x + 1, k]
-        if x >= 3:
-            v = v + xm[1, x - 3, k]
+        v = mb[field(x + 1, k)]
+        if x == -1:
+            v = v + xm[0, field(1, k) - 5]
+        if x == 0:
+            v = v + xm[0, field(1, 0 if k == 1 else k)]
+        if x == 3:
+            v = v - xm[1, 0] if k == 1 else v + xm[1, field(0, k) - 2]
+        if x == 4:
+            v = v + xm[1, field(1, k) - 2]
         d = 8 * (9 + k) + x + 2
         v = v + jnp.where(first, rolly(exl, -d), 0.0)
         v = v + jnp.where(last, rolly(exr, 127 - d), 0.0)
         m.append(v)
-    w = xm[0, 0, 4] if x < 0 else xm[1, 1, 4] if x == ROWS else mb[x + 1, 4]
+    w = xm[0, 4] if x < 0 else xm[1, 7] if x == ROWS else mb[field(x + 1, 4)]
     g = []
     for q, (cx, cy, cz) in enumerate(Q):
         v = source(q, x + cx)
@@ -246,15 +259,15 @@
         if cy == -1:
             v = jnp.where(first, rolly(gy[q], -d), rolly(v, 1))
         g.append(rollz(v, -cz))
-    got = pull_back(g, [uck[x, k] for k in range(3)], rates, mb[x + 1, 4])
+    got = pull_back(g, [uck[x, k] for k in range(3)], rates, mb[field(x + 1, 4)])
     for q in range(27):
         out[q] = got[q]
 
 
 def exchange(
     sizes, ck_hbm, cot_hbm, wall_hbm, rates_hbm,
-    cot, mb, ey, uck, rv, xc, xm, xe, en, upper, done,
-    ck, wall, rates_ref, ehi, gy, load, ready, send, recv,
+    cot, mb, uck, rv, xc, xm, upper, gy, done, beside,
+    ck, wall, rates_ref, ey, eh, el, en, ep, load, ready, send, recv,
 ):
     nx, ny = sizes
     lane = lanes()
@@ -269,17 +282,33 @@
         for dy in (0, 1, -1):
             pl.semaphore_signal(sem, inc=1, device_id=device(dx, dy), device_id_type=MESH)
 
+    place = lax.rem(lax.axis_index("gx"), nx // 2)
+    opens, closes = place == 0, place == nx // 2 - 1
     barrier = pltpu.get_barrier_semaphore()
     signal(barrier, -1)
+
+    @pl.when(jnp.logical_not(closes))
+    def _():
+        for dy in (1, -1):
+            pl.semaphore_signal(barrier, inc=1, device_id=device(0, dy), device_id_type=MESH)
+
     loads = []
     for src, dst in ((cot_hbm.reshape(864, 128), cot), (ck_hbm, ck), (wall_hbm, wall), (rates_hbm, rates_ref)):
         loads.append(pltpu.make_async_copy(src, dst, load.at[len(loads)]))
         loads[-1].start()
-    pl.semaphore_wait(barrier, 3)
+
+    @pl.when(closes)
+    def _():
+        pl.semaphore_wait(barrier, 3)
+
+    @pl.when(jnp.logical_not(closes))
+    def _():
+        pl.semaphore_wait(barrier, 5)
+
 
     copies, late, soon = [], [], []
 
-    def put(src, dst, dx, dy):
+    def copy_to(src, dst, dx, dy):
         n = len(copies)
         copies.append(
             pltpu.make_async_remote_copy(
@@ -291,11 +320,13 @@
                 device_id_type=MESH,
             )
         )
-        copies[-1].start()
         (late if dx == 1 else soon).append(copies[-1])
+        return copies[-1]
+
+    def put(src, dst, dx, dy):
+        copy_to(src, dst, dx, dy).start()
 
     put(cot_hbm.at[pl.ds(0, 18), :, 3], xc.at[0, pl.ds(0, 18)], 1, 0)
-    put(cot_hbm.at[pl.ds(0, 9), :, 2], xc.at[0, pl.ds(18, 9)], 1, 0)
     signal(ready, 1)
     loads[0].wait()
 
@@ -339,17 +370,14 @@
         add("r1", v, d)
         add("l1", v, d + 1)
 
-    def store_packs(ref):
-        ref[0, 0] = acc["l0"] + rolly(acc["l0m"], 1)
-        ref[1, 0] = rolly(acc["l1"], -1)
-        ref[2, 0] = rolly(acc["l2"], -1)
-        ref[0, 1] = acc["r0"]
-        ref[1, 1] = acc["r1"]
-        ref[2, 1] = rolly(acc["r2"], 1)
+    def packed():
+        left = acc["l0"] + rolly(acc["l0m"], 1), rolly(acc["l1"], -1), rolly(acc["l2"], -1)
+        right = acc["r0"], acc["r1"], rolly(acc["r2"], 1)
+        return left, right
 
     def collide_row(x):
         w = wall_row(wall, x)
-        mb[x + 1, 4] = w
+        mb[field(x + 1, 4)] = w
         pack_wall(x, w)
         out, u = collide([row(ck, q, x) for q in range(27)], rates, w)
         for k in range(3):
@@ -379,7 +407,7 @@
 
     def store_sums(r):
         for k in range(4):
-            mb[r, k] = body[r][k]
+            mb[field(r, k)] = body[r][k]
         pack_sums(r)
 
     pack_cotangent(3)
@@ -387,34 +415,61 @@
     for c in loads[1:]:
         c.wait()
     rates = halved_rates(rates_ref)
-    mb[5, 4] = zero
     collide_row(3)
     collide_row(2)
     store_sums(5)
     store_sums(4)
-    store_packs(ehi)
-    put(ehi.at[:, 1], en.at[1], 1, 1)
-    put(ehi.at[:, 0], en.at[4], 1, -1)
-    put(mb.at[pl.ds(4, 2)], xm.at[0], 1, 0)
-    put(ehi.at[0], xe.at[0], 1, 0)
-
-    mb[0, 4] = zero
+    left, right = packed()
+    eh[0] = right[0] + (rolly(right[1], -3) + rolly(right[2], 3))
+    eh[1] = left[0] + (rolly(left[1], -3) + rolly(left[2], 3))
+    eh[2] = left[0] + rolly(right[0], -3)
+    put(eh.at[0], ep.at[0], 1, 1)
+    put(eh.at[1], ep.at[1], 1, -1)
+    put(eh.at[2], ep.at[2], 1, 0)
+    put(mb.at[pl.ds(20, 8)], xm.at[0], 1, 0)
+    put(cot_hbm.at[pl.ds(0, 9), :, 2], xc.at[0, pl.ds(18, 9)], 1, 0)
+
     pack_cotangent(1)
     pack_cotangent(0)
     collide_row(1)
     collide_row(0)
     for r in range(4):
         store_sums(r)
-    store_packs(ey)
-    pl.semaphore_wait(ready, 3)
-    put(cot_hbm.at[pl.ds(9, 18), :, 0], xc.at[1, pl.ds(0, 18)], -1, 0)
-    put(cot_hbm.at[pl.ds(18, 9), :, 1], xc.at[1, pl.ds(18, 9)], -1, 0)
-    put(ey.at[:, 1], en.at[2], -1, 1)
-    put(ey.at[:, 0], en.at[5], -1, -1)
-    put(mb.at[pl.ds(0, 2)], xm.at[1], -1, 0)
-    put(ey.at[0], xe.at[1], -1, 0)
+    left, right = packed()
+    for k in range(3):
+        ey[k, 0] = left[k]
+        ey[k, 1] = right[k]
+    rest = (lane % 8 > 0) & (lane % 8 < 4)
+    left = [jnp.where(rest, v, 0.0) for v in left]
+    right = [jnp.where(rest, v, 0.0) for v in right]
+    el[0] = right[0] + (rolly(right[1], 3) + rolly(right[2], 5))
+    el[1] = left[0] + (rolly(left[1], 3) + rolly(left[2], 5))
+    el[2] = left[0] + rolly(right[0], 3)
+
+    @pl.when(closes)
+    def _():
+        pl.semaphore_wait(ready, 3)
+
     put(ey.at[:, 1], en.at[0], 0, 1)
-    put(ey.at[:, 0], en.at[3], 0, -1)
+    put(ey.at[:, 0], en.at[1], 0, -1)
+    back = [
+        copy_to(cot_hbm.at[pl.ds(9, 18), :, 0], xc.at[1, pl.ds(0, 18)], -1, 0),
+        copy_to(el.at[0], ep.at[3], -1, 1),
+        copy_to(el.at[1], ep.at[4], -1, -1),
+        copy_to(el.at[2], ep.at[5], -1, 0),
+        copy_to(mb.at[pl.ds(2, 8)], xm.at[1], -1, 0),
+        copy_to(cot_hbm.at[pl.ds(18, 9), :, 1], xc.at[1, pl.ds(18, 9)], -1, 0),
+    ]
+
+    @pl.when(jnp.logical_not(opens | closes))
+    def _():
+        pl.semaphore_wait(ready, 3)
+
+    @pl.when(jnp.logical_not(opens))
+    def _():
+        for c in back:
+            c.start()
+
     for n in range(27):
         rv[n] = jnp.full((8, 128), rates[n], F32)
 
@@ -424,24 +479,42 @@
     def known(n):
         return rv[n]
 
-    packs = merged(en, ey, xe, False)
+    def gn(x):
+        return upper.at[x]
+
+    packs = merged(en, ep, ey, False)
+    exl, exr = packs[0][0], packs[1][0]
     for x in (4, 3, 2, 1):
-        pull_row(x, packs, known, cot, mb, xc, xm, upper.at[x - 1])
+        pull_row(x, exl, exr, known, cot, mb, xc, xm, gn(x))
     pull_beside(packs, known, gy)
     for x in (3, 2):
-        pull_first(x, known, uck, mb, lambda x: upper.at[x - 1], gy, done.at[x - 2])
-    for c in late:
+        pull_first(x, known, uck, mb, gn, gy, done.at[x - 1])
+
+    @pl.when(opens)
+    def _():
+        pl.semaphore_wait(ready, 3)
+        for c in back:
+            c.start()
+
+    for c in late[:-1]:
         c.wait_recv()
+    packs = merged(en, ep, ey, True)
+    exl, exr = packs[0][0], packs[1][0]
+    beside[0], beside[1] = exl, exr
+    pull_row(0, exl, exr, known, cot, mb, xc, xm, gn(0))
+    pull_beside(packs, known, gy)
+    pull_first(1, known, uck, mb, gn, gy, done.at[0])
+    late[-1].wait_recv()
     for c in copies:
         c.wait_send()
 
 
-def finish(cot, mb, ey, uck, rv, xc, xm, xe, en, upper, done, out, lower, gy, ends, sems):
+def finish(cot, mb, uck, rv, xc, xm, upper, gy, done, beside, out, lower, end, sems):
     def rates(n):
         return rv[n]
 
     def gn(x):
-        return lower.at[x + 1] if x <= 0 else upper.at[x - 1]
+        return lower if x < 0 else upper.at[x]
 
     copies = []
 
@@ -449,16 +522,11 @@
         copies.append(pltpu.make_async_copy(src, out.at[:, :, x], sems.at[x]))
         copies[-1].start()
 
-    put(done.at[0], 2)
-    put(done.at[1], 3)
-    packs = merged(en, ey, xe, True)
-    pull_beside(packs, rates, gy)
-    pull_row(0, packs, rates, cot, mb, xc, xm, gn(0))
-    pull_first(1, rates, uck, mb, gn, gy, ends.at[1])
-    put(ends.at[1], 1)
-    pull_row(-1, packs, rates, cot, mb, xc, xm, gn(-1))
-    pull_first(0, rates, uck, mb, gn, gy, ends.at[0])
-    put(ends.at[0], 0)
+    for x in (1, 2, 3):
+        put(done.at[x - 1], x)
+    pull_row(-1, beside[0], beside[1], rates, cot, mb, xc, xm, lower)
+    pull_first(0, rates, uck, mb, gn, gy, end)
+    put(end, 0)
     for c in copies:
         c.wait()
 
@@ -475,18 +543,20 @@
     got = pl.pallas_call(
         functools.partial(exchange, sizes),
         out_shape=(
-            like(864, 128), like(6, 5, 8, 128), like(3, 2, 8, 128), like(4, 3, 8, 128), like(27, 8, 128),
-            like(2, 27, 8, 128), like(2, 2, 5, 8, 128), like(2, 2, 8, 128), like(6, 3, 8, 128),
-            like(4, 27, 8, 128), like(2, 27, 8, 128),
+            like(864, 128), like(30, 8, 128), like(4, 3, 8, 128), like(27, 8, 128), like(2, 27, 8, 128),
+            like(2, 8, 8, 128), like(5, 27, 8, 128), like(27, 8, 128), like(3, 27, 8, 128), like(2, 8, 128),
         ),
         in_specs=[hbm] * 4,
-        out_specs=(vmem,) * 11,
+        out_specs=(vmem,) * 10,
         scratch_shapes=[
             pltpu.VMEM((864, 128), F32),
             pltpu.VMEM((32, 128), jnp.int32),
             pltpu.SMEM((1, 27), F32),
             pltpu.VMEM((3, 2, 8, 128), F32),
-            pltpu.VMEM((27, 8, 128), F32),
+            pltpu.VMEM((3, 8, 128), F32),
+            pltpu.VMEM((3, 8, 128), F32),
+            pltpu.VMEM((2, 3, 8, 128), F32),
+            pltpu.VMEM((6, 8, 128), F32),
             pltpu.SemaphoreType.DMA((4,)),
             pltpu.SemaphoreType.REGULAR,
             pltpu.SemaphoreType.DMA((14,)),
@@ -498,12 +568,11 @@
     return pl.pallas_call(
         finish,
         out_shape=like(27, 8, 4, 128),
-        in_specs=[vmem] * 11,
+        in_specs=[vmem] * 10,
         out_specs=hbm,
         scratch_shapes=[
-            pltpu.VMEM((2, 27, 8, 128), F32),
             pltpu.VMEM((27, 8, 128), F32),
-            pltpu.VMEM((2, 27, 8, 128), F32),
+            pltpu.VMEM((27, 8, 128), F32),
             pltpu.SemaphoreType.DMA((4,)),
         ],
         compiler_params=pltpu.CompilerParams(**small),

time: 20.5 us -> 19.9 us (0.971)
  Pallas kernels: 20.4 us -> 19.7 us
    pallas_call x1, Pallas kernels: 19.2 us -> 18.8 us  [shards(): pl.pallas_call(functools.partial(exchange, sizes), out_shape=(like(864, 1...]
    pallas_call x1, Pallas kernels: 1.18 us -> 0.94 us  [shards(): pl.pallas_call(finish, out_shape=like(27, 8, 4, 128), in_specs=[vmem] * 1...]
where the time goes in v4:
time: 19.9 us; the launch traced here: 19.7 us
  Pallas kernels  19.7 us (99%)
    pallas_call x1, Pallas kernels, shards(): pl.pallas_call(functools.partial(exchange, sizes), out_shape=(like(864, 1...  18.8 us
    pallas_call x1, Pallas kernels, shards(): pl.pallas_call(finish, out_shape=like(27, 8, 4, 128), in_specs=[vmem] * 1...  0.94 us

profile of v4, /device:TPU:1, one launch (start us, length us, event | category | flops | bytes accessed | tf_op | source)
XLA Modules:
  0.0 19.7 jit_solution(518775055386383670)
XLA Ops:
  0.0 18.8 %exchange.1 = (f32[864,128]{1,0:T(8,128)S(1)}, f32[30,8,128]{2,1,0:T(8,128)S(1)}, f32[4,3,8,128]{3,2,1,0:T(8,128)S(1)}, f32[27,8,128]{2,1,0:T(8,128)S(1)}, f32[2...) custom-call(f32[864,128]{1,0:T(8,128)} %bitcast.3, ...), custom_call_target="tpu_custom_call" | custom-call | tf_op jit(solution)/shard_map/exchange/pallas_call | solution.py:543
  18.8 0.9 %finish.1 = f32[27,8,4,128]{3,2,1,0:T(4,128)} custom-call(f32[864,128]{1,0:T(8,128)S(1)} %get-tuple-element.15.cot, f32[30,8,128]{2,1,0:T(8,128)S(1)} %get-tuple-element.16.mb, f32[4,3,8,128]{3,2,1,0:T(8,128)S(1)} %get-tuple-element.17.uck, f32[27,8,128]{2,1,0:T(8,128)S(1)} %get-tuple-element.18.rv, f32[2,27,8,128]{3,2,1,0:T(8,128)S(1)} %get-tuple-element.19.xc, ...), custom_call_target="tpu_custom_call" | custom-call | tf_op jit(solution)/shard_map/finish/pallas_call | solution.py:568

commit v5 on v4

--- a/solution.py
+++ b/solution.py
@@ -267,7 +267,7 @@
 def exchange(
     sizes, ck_hbm, cot_hbm, wall_hbm, rates_hbm,
     cot, mb, uck, rv, xc, xm, upper, gy, done, beside,
-    ck, wall, rates_ref, ey, eh, el, en, ep, load, ready, send, recv,
+    ck, wall, rates_ref, ey, eh, el, sh, sl, en, ep, load, straight, aslant, send, recv,
 ):
     nx, ny = sizes
     lane = lanes()
@@ -278,19 +278,18 @@
             lax.rem(lax.axis_index("gy") + (dy + ny), ny),
         )
 
-    def signal(sem, dx):
-        for dy in (0, 1, -1):
+    def signal(sem, dx, steps):
+        for dy in steps:
             pl.semaphore_signal(sem, inc=1, device_id=device(dx, dy), device_id_type=MESH)
 
     place = lax.rem(lax.axis_index("gx"), nx // 2)
     opens, closes = place == 0, place == nx // 2 - 1
     barrier = pltpu.get_barrier_semaphore()
-    signal(barrier, -1)
+    signal(barrier, -1, (0, 1, -1))
 
     @pl.when(jnp.logical_not(closes))
     def _():
-        for dy in (1, -1):
-            pl.semaphore_signal(barrier, inc=1, device_id=device(0, dy), device_id_type=MESH)
+        signal(barrier, 0, (1, -1))
 
     loads = []
     for src, dst in ((cot_hbm.reshape(864, 128), cot), (ck_hbm, ck), (wall_hbm, wall), (rates_hbm, rates_ref)):
@@ -326,9 +325,13 @@
     def put(src, dst, dx, dy):
         copy_to(src, dst, dx, dy).start()
 
-    put(cot_hbm.at[pl.ds(0, 18), :, 3], xc.at[0, pl.ds(0, 18)], 1, 0)
-    signal(ready, 1)
+    put(cot_hbm.at[pl.ds(0, 9), :, 3], xc.at[0, pl.ds(0, 9)], 1, 0)
+    signal(straight, 1, (0,))
+    signal(aslant, 1, (1, -1))
     loads[0].wait()
+    for q in range(9):
+        sh[q] = row(cot, q + 9, 3)
+        sh[q + 9] = row(cot, q, 2)
 
     zero = jnp.zeros((8, 128), F32)
     first, last = lane == 0, lane == 127
@@ -427,7 +430,7 @@
     put(eh.at[1], ep.at[1], 1, -1)
     put(eh.at[2], ep.at[2], 1, 0)
     put(mb.at[pl.ds(20, 8)], xm.at[0], 1, 0)
-    put(cot_hbm.at[pl.ds(0, 9), :, 2], xc.at[0, pl.ds(18, 9)], 1, 0)
+    put(sh, xc.at[0, pl.ds(9, 18)], 1, 0)
 
     pack_cotangent(1)
     pack_cotangent(0)
@@ -446,29 +449,41 @@
     el[1] = left[0] + (rolly(left[1], 3) + rolly(left[2], 5))
     el[2] = left[0] + rolly(right[0], 3)
 
+    for q in range(18):
+        sl[q] = row(cot, q + 9, 0)
+    for q in range(9):
+        sl[q + 18] = row(cot, q + 18, 1)
+
     @pl.when(closes)
     def _():
-        pl.semaphore_wait(ready, 3)
+        pl.semaphore_wait(straight, 1)
 
     put(ey.at[:, 1], en.at[0], 0, 1)
     put(ey.at[:, 0], en.at[1], 0, -1)
-    back = [
-        copy_to(cot_hbm.at[pl.ds(9, 18), :, 0], xc.at[1, pl.ds(0, 18)], -1, 0),
+    slanting = [
         copy_to(el.at[0], ep.at[3], -1, 1),
         copy_to(el.at[1], ep.at[4], -1, -1),
+    ]
+    back = [
         copy_to(el.at[2], ep.at[5], -1, 0),
         copy_to(mb.at[pl.ds(2, 8)], xm.at[1], -1, 0),
-        copy_to(cot_hbm.at[pl.ds(18, 9), :, 1], xc.at[1, pl.ds(18, 9)], -1, 0),
+        copy_to(sl, xc.at[1], -1, 0),
     ]
 
     @pl.when(jnp.logical_not(opens | closes))
     def _():
-        pl.semaphore_wait(ready, 3)
+        pl.semaphore_wait(straight, 1)
+
+    def send_back():
+        for c in back:
+            c.start()
+        pl.semaphore_wait(aslant, 2)
+        for c in slanting:
+            c.start()
 
     @pl.when(jnp.logical_not(opens))
     def _():
-        for c in back:
-            c.start()
+        send_back()
 
     for n in range(27):
         rv[n] = jnp.full((8, 128), rates[n], F32)
@@ -492,9 +507,8 @@
 
     @pl.when(opens)
     def _():
-        pl.semaphore_wait(ready, 3)
-        for c in back:
-            c.start()
+        pl.semaphore_wait(straight, 1)
+        send_back()
 
     for c in late[:-1]:
         c.wait_recv()
@@ -555,12 +569,15 @@
             pltpu.VMEM((3, 2, 8, 128), F32),
             pltpu.VMEM((3, 8, 128), F32),
             pltpu.VMEM((3, 8, 128), F32),
+            pltpu.VMEM((18, 8, 128), F32),
+            pltpu.VMEM((27, 8, 128), F32),
             pltpu.VMEM((2, 3, 8, 128), F32),
             pltpu.VMEM((6, 8, 128), F32),
             pltpu.SemaphoreType.DMA((4,)),
             pltpu.SemaphoreType.REGULAR,
-            pltpu.SemaphoreType.DMA((14,)),
-            pltpu.SemaphoreType.DMA((14,)),
+            pltpu.SemaphoreType.REGULAR,
+            pltpu.SemaphoreType.DMA((13,)),
+            pltpu.SemaphoreType.DMA((13,)),
         ],
         compiler_params=pltpu.CompilerParams(collective_id=0, has_side_effects=True, **small),
         name="exchange",

time: 19.9 us -> 19.6 us (0.985)
  Pallas kernels: 19.7 us -> 19.4 us
    pallas_call x1, Pallas kernels: 18.8 us -> 18.5 us  [shards(): pl.pallas_call(functools.partial(exchange, sizes), out_shape=(like(864, 1...]
where the time goes in v5:
time: 19.6 us; the launch traced here: 19.4 us
  Pallas kernels  19.4 us (99%)
    pallas_call x1, Pallas kernels, shards(): pl.pallas_call(functools.partial(exchange, sizes), out_shape=(like(864, 1...  18.5 us
    pallas_call x1, Pallas kernels, shards(): pl.pallas_call(finish, out_shape=like(27, 8, 4, 128), in_specs=[vmem] * 1...  0.94 us

profile of v5, /device:TPU:1, one launch (start us, length us, event | category | flops | bytes accessed | tf_op | source)
XLA Modules:
  0.0 19.4 jit_solution(3266795005350778805)
XLA Ops:
  0.0 18.5 %exchange.1 = (f32[864,128]{1,0:T(8,128)S(1)}, f32[30,8,128]{2,1,0:T(8,128)S(1)}, f32[4,3,8,128]{3,2,1,0:T(8,128)S(1)}, f32[27,8,128]{2,1,0:T(8,128)S(1)}, f32[2...) custom-call(f32[864,128]{1,0:T(8,128)} %bitcast.3, ...), custom_call_target="tpu_custom_call" | custom-call | tf_op jit(solution)/shard_map/exchange/pallas_call | solution.py:557
  18.5 0.9 %finish.1 = f32[27,8,4,128]{3,2,1,0:T(4,128)} custom-call(f32[864,128]{1,0:T(8,128)S(1)} %get-tuple-element.15.cot, f32[30,8,128]{2,1,0:T(8,128)S(1)} %get-tuple-element.16.mb, f32[4,3,8,128]{3,2,1,0:T(8,128)S(1)} %get-tuple-element.17.uck, f32[27,8,128]{2,1,0:T(8,128)S(1)} %get-tuple-element.18.rv, f32[2,27,8,128]{3,2,1,0:T(8,128)S(1)} %get-tuple-element.19.xc, ...), custom_call_target="tpu_custom_call" | custom-call | tf_op jit(solution)/shard_map/finish/pallas_call | solution.py:585

commit v6 on v5

--- a/solution.py
+++ b/solution.py
@@ -282,6 +282,21 @@
         for dy in steps:
             pl.semaphore_signal(sem, inc=1, device_id=device(dx, dy), device_id_type=MESH)
 
+    loads = []
+    for src, dst in (
+        (cot_hbm.at[pl.ds(0, 18), :, 3], sh.at[pl.ds(0, 18)]),
+        (cot_hbm.at[pl.ds(0, 9), :, 2], sh.at[pl.ds(18, 9)]),
+        (ck_hbm.at[:, :, 3], ck.at[3]),
+        (ck_hbm.at[:, :, 2], ck.at[2]),
+        (wall_hbm, wall),
+        (rates_hbm, rates_ref),
+        (cot_hbm.reshape(864, 128), cot),
+        (ck_hbm.at[:, :, 1], ck.at[1]),
+        (ck_hbm.at[:, :, 0], ck.at[0]),
+    ):
+        loads.append(pltpu.make_async_copy(src, dst, load.at[len(loads)]))
+        loads[-1].start()
+
     place = lax.rem(lax.axis_index("gx"), nx // 2)
     opens, closes = place == 0, place == nx // 2 - 1
     barrier = pltpu.get_barrier_semaphore()
@@ -290,11 +305,6 @@
     @pl.when(jnp.logical_not(closes))
     def _():
         signal(barrier, 0, (1, -1))
-
-    loads = []
-    for src, dst in ((cot_hbm.reshape(864, 128), cot), (ck_hbm, ck), (wall_hbm, wall), (rates_hbm, rates_ref)):
-        loads.append(pltpu.make_async_copy(src, dst, load.at[len(loads)]))
-        loads[-1].start()
 
     @pl.when(closes)
     def _():
@@ -328,11 +338,6 @@
     put(cot_hbm.at[pl.ds(0, 9), :, 3], xc.at[0, pl.ds(0, 9)], 1, 0)
     signal(straight, 1, (0,))
     signal(aslant, 1, (1, -1))
-    loads[0].wait()
-    for q in range(9):
-        sh[q] = row(cot, q + 9, 3)
-        sh[q + 9] = row(cot, q, 2)
-
     zero = jnp.zeros((8, 128), F32)
     first, last = lane == 0, lane == 127
     body = [[zero] * 4 for _ in range(6)]
@@ -342,16 +347,16 @@
     def add(name, v, d):
         acc[name] = jnp.where(lane == d, v, acc[name])
 
-    def pack_cotangent(x):
-        for i, (cx, cz) in enumerate([(a, c) for a in range(3) for c in range(3)]):
-            d = 8 * i + x + 2
-            v = rolly(row(cot, at(cx, 0, cz), x), d - 127)
+    def pack_cotangent(x, steps, get):
+        for cx, cz in [(a, c) for a in steps for c in range(3)]:
+            d = 8 * (3 * cx + cz) + x + 2
+            v = rolly(get(at(cx, 0, cz)), d - 127)
             add("r0", v, d)
             add("r2", v, d - 1)
-            v = rolly(row(cot, at(cx, 2, cz), x), d)
+            v = rolly(get(at(cx, 2, cz)), d)
             add("l0", v, d)
             add("l2", v, d + 1)
-            v = rolly(row(cot, at(cx, 1, cz), x), d - 127)
+            v = rolly(get(at(cx, 1, cz)), d - 127)
             add("r1", v, d)
             add("l1", v, d + 1)
 
@@ -382,7 +387,7 @@
         w = wall_row(wall, x)
         mb[field(x + 1, 4)] = w
         pack_wall(x, w)
-        out, u = collide([row(ck, q, x) for q in range(27)], rates, w)
+        out, u = collide([ck[x, q] for q in range(27)], rates, w)
         for k in range(3):
             uck[x, k] = u[k]
         for a in range(3):
@@ -413,10 +418,10 @@
             mb[field(r, k)] = body[r][k]
         pack_sums(r)
 
-    pack_cotangent(3)
-    pack_cotangent(2)
-    for c in loads[1:]:
+    for c in loads[:6]:
         c.wait()
+    pack_cotangent(3, (0, 1), lambda q: sh[q])
+    pack_cotangent(2, (0,), lambda q: sh[q + 18])
     rates = halved_rates(rates_ref)
     collide_row(3)
     collide_row(2)
@@ -430,10 +435,12 @@
     put(eh.at[1], ep.at[1], 1, -1)
     put(eh.at[2], ep.at[2], 1, 0)
     put(mb.at[pl.ds(20, 8)], xm.at[0], 1, 0)
-    put(sh, xc.at[0, pl.ds(9, 18)], 1, 0)
-
-    pack_cotangent(1)
-    pack_cotangent(0)
+    put(sh.at[pl.ds(9, 18)], xc.at[0, pl.ds(9, 18)], 1, 0)
+
+    for c in loads[6:]:
+        c.wait()
+    for x, steps in ((3, (2,)), (2, (1, 2)), (1, range(3)), (0, range(3))):
+        pack_cotangent(x, steps, lambda q: row(cot, q, x))
     collide_row(1)
     collide_row(0)
     for r in range(4):
@@ -546,7 +553,6 @@
 
 
 def shards(sizes, checkpoint, rates, wall_mask, cotangent):
-    ck = checkpoint.reshape(864, 128)
     wall, rates = wall_mask.reshape(32, 128), rates.reshape(1, 27)
     vmem, hbm = pl.BlockSpec(memory_space=pltpu.VMEM), pl.BlockSpec(memory_space=pltpu.HBM)
     small = dict(vmem_limit_bytes=16 << 20)
@@ -563,17 +569,17 @@
         in_specs=[hbm] * 4,
         out_specs=(vmem,) * 10,
         scratch_shapes=[
-            pltpu.VMEM((864, 128), F32),
+            pltpu.VMEM((4, 27, 8, 128), F32),
             pltpu.VMEM((32, 128), jnp.int32),
             pltpu.SMEM((1, 27), F32),
             pltpu.VMEM((3, 2, 8, 128), F32),
             pltpu.VMEM((3, 8, 128), F32),
             pltpu.VMEM((3, 8, 128), F32),
-            pltpu.VMEM((18, 8, 128), F32),
+            pltpu.VMEM((27, 8, 128), F32),
             pltpu.VMEM((27, 8, 128), F32),
             pltpu.VMEM((2, 3, 8, 128), F32),
             pltpu.VMEM((6, 8, 128), F32),
-            pltpu.SemaphoreType.DMA((4,)),
+            pltpu.SemaphoreType.DMA((9,)),
             pltpu.SemaphoreType.REGULAR,
             pltpu.SemaphoreType.REGULAR,
             pltpu.SemaphoreType.DMA((13,)),
@@ -581,7 +587,7 @@
         ],
         compiler_params=pltpu.CompilerParams(collective_id=0, has_side_effects=True, **small),
         name="exchange",
-    )(*[pltpu.with_memory_space_constraint(v, pltpu.HBM) for v in (ck, cotangent, wall, rates)])
+    )(*[pltpu.with_memory_space_constraint(v, pltpu.HBM) for v in (checkpoint, cotangent, wall, rates)])
     return pl.pallas_call(
         finish,
         out_shape=like(27, 8, 4, 128),

time: 19.6 us -> 19.4 us (0.990)
  no operation moved by 1% of the time
where the time goes in v6:
time: 19.4 us; the launch traced here: 19.3 us
  Pallas kernels  19.3 us (99%)
    pallas_call x1, Pallas kernels, shards(): pl.pallas_call(functools.partial(exchange, sizes), out_shape=(like(864, 1...  18.3 us
    pallas_call x1, Pallas kernels, shards(): pl.pallas_call(finish, out_shape=like(27, 8, 4, 128), in_specs=[vmem] * 1...  0.94 us

profile of v6, /device:TPU:1, one launch (start us, length us, event | category | flops | bytes accessed | tf_op | source)
XLA Modules:
  0.0 19.3 jit_solution(15015133822744738691)
XLA Ops:
  0.0 18.3 %exchange.1 = (f32[864,128]{1,0:T(8,128)S(1)}, f32[30,8,128]{2,1,0:T(8,128)S(1)}, f32[4,3,8,128]{3,2,1,0:T(8,128)S(1)}, f32[27,8,128]{2,1,0:T(8,128)S(1)}, f32[2...) custom-call(f32[27,8,4,128]{3,2,1,0:T(4,128)} %ck_hbm.1, ...), custom_call_target="tpu_custom_call" | custom-call | tf_op jit(solution)/shard_map/exchange/pallas_call | solution.py:563
  18.3 0.9 %finish.1 = f32[27,8,4,128]{3,2,1,0:T(4,128)} custom-call(f32[864,128]{1,0:T(8,128)S(1)} %get-tuple-element.15.cot, f32[30,8,128]{2,1,0:T(8,128)S(1)} %get-tuple-element.16.mb, f32[4,3,8,128]{3,2,1,0:T(8,128)S(1)} %get-tuple-element.17.uck, f32[27,8,128]{2,1,0:T(8,128)S(1)} %get-tuple-element.18.rv, f32[2,27,8,128]{3,2,1,0:T(8,128)S(1)} %get-tuple-element.19.xc, ...), custom_call_target="tpu_custom_call" | custom-call | tf_op jit(solution)/shard_map/finish/pallas_call | solution.py:591

commit v7 on v6

--- a/solution.py
+++ b/solution.py
@@ -195,7 +195,8 @@
         s = 9 + k
         m.append(jnp.where(left, rolly(lo, -8 * s), rolly(hi, 8 - 8 * s)))
     w = jnp.where(left, rolly(exl[1], -104), rolly(exr[1], -96))
-    inv = 1.0 / jnp.where(m[0] > 0.0, m[0], 1.0)
+    cell = (lane < 16) & (lane % 8 > 0) & (lane % 8 < 7)
+    inv = 1.0 / jnp.where(cell, m[0], 1.0)
     got = pull_back(g, [m[k] * inv for k in (1, 2, 3)], rates, w)
     for q, (cx, cy, cz) in enumerate(Q):
         if cy != 0:
@@ -284,12 +285,12 @@
 
     loads = []
     for src, dst in (
+        (rates_hbm, rates_ref),
+        (wall_hbm, wall),
+        (ck_hbm.at[:, :, 3], ck.at[3]),
+        (ck_hbm.at[:, :, 2], ck.at[2]),
         (cot_hbm.at[pl.ds(0, 18), :, 3], sh.at[pl.ds(0, 18)]),
         (cot_hbm.at[pl.ds(0, 9), :, 2], sh.at[pl.ds(18, 9)]),
-        (ck_hbm.at[:, :, 3], ck.at[3]),
-        (ck_hbm.at[:, :, 2], ck.at[2]),
-        (wall_hbm, wall),
-        (rates_hbm, rates_ref),
         (cot_hbm.reshape(864, 128), cot),
         (ck_hbm.at[:, :, 1], ck.at[1]),
         (ck_hbm.at[:, :, 0], ck.at[0]),
@@ -431,8 +432,8 @@
     eh[0] = right[0] + (rolly(right[1], -3) + rolly(right[2], 3))
     eh[1] = left[0] + (rolly(left[1], -3) + rolly(left[2], 3))
     eh[2] = left[0] + rolly(right[0], -3)
+    put(eh.at[1], ep.at[1], 1, -1)
     put(eh.at[0], ep.at[0], 1, 1)
-    put(eh.at[1], ep.at[1], 1, -1)
     put(eh.at[2], ep.at[2], 1, 0)
     put(mb.at[pl.ds(20, 8)], xm.at[0], 1, 0)
     put(sh.at[pl.ds(9, 18)], xc.at[0, pl.ds(9, 18)], 1, 0)

time: 19.4 us -> 19.3 us (level)
  no operation moved by 1% of the time
where the time goes in v7:
time: 19.3 us; the launch traced here: 19.2 us
  Pallas kernels  19.2 us (99%)
    pallas_call x1, Pallas kernels, shards(): pl.pallas_call(functools.partial(exchange, sizes), out_shape=(like(864, 1...  18.3 us
    pallas_call x1, Pallas kernels, shards(): pl.pallas_call(finish, out_shape=like(27, 8, 4, 128), in_specs=[vmem] * 1...  0.94 us

profile of v7, /device:TPU:1, one launch (start us, length us, event | category | flops | bytes accessed | tf_op | source)
XLA Modules:
  0.0 19.2 jit_solution(13667546961173183314)
XLA Ops:
  0.0 18.3 %exchange.1 = (f32[864,128]{1,0:T(8,128)S(1)}, f32[30,8,128]{2,1,0:T(8,128)S(1)}, f32[4,3,8,128]{3,2,1,0:T(8,128)S(1)}, f32[27,8,128]{2,1,0:T(8,128)S(1)}, f32[2...) custom-call(f32[27,8,4,128]{3,2,1,0:T(4,128)} %ck_hbm.1, ...), custom_call_target="tpu_custom_call" | custom-call | tf_op jit(solution)/shard_map/exchange/pallas_call | solution.py:564
  18.3 0.9 %finish.1 = f32[27,8,4,128]{3,2,1,0:T(4,128)} custom-call(f32[864,128]{1,0:T(8,128)S(1)} %get-tuple-element.15.cot, f32[30,8,128]{2,1,0:T(8,128)S(1)} %get-tuple-element.16.mb, f32[4,3,8,128]{3,2,1,0:T(8,128)S(1)} %get-tuple-element.17.uck, f32[27,8,128]{2,1,0:T(8,128)S(1)} %get-tuple-element.18.rv, f32[2,27,8,128]{3,2,1,0:T(8,128)S(1)} %get-tuple-element.19.xc, ...), custom_call_target="tpu_custom_call" | custom-call | tf_op jit(solution)/shard_map/finish/pallas_call | solution.py:592

commit v8 on v7

--- a/solution.py
+++ b/solution.py
@@ -150,23 +150,25 @@
     return jnp.where((height == 0) | (height == 7), 1, mask).astype(F32)
 
 
-def merged(en, ep, ey, below):
-    lane = lanes() % 8
-
-    def ends(v, k, low):
-        if low:
-            return jnp.where(lane < (2 if k == 2 else 3), rolly(v, (-4, -1, -7)[k]), 0.0)
-        return jnp.where(lane >= (6 if k == 2 else 5), rolly(v, (4, 1, -1)[k]), 0.0)
-
-    def merge(own, k, which):
-        own = own + ends(ep[3 + which], k, False)
-        return own + ends(ep[which], k, True) if below else own
-
-    exl = [merge(en[0, k], k, 0) for k in range(3)]
-    exr = [merge(en[1, k], k, 1) for k in range(3)]
-    oxl = merge(ey[0, 0], 0, 2)
-    oxr = merge(ey[0, 1], 1, 2)
-    return exl, exr, oxl, oxr
+def upper_end(v, k):
+    return jnp.where(lanes() % 8 >= (6 if k == 2 else 5), rolly(v, (4, 1, -1)[k]), 0.0)
+
+
+def lower_end(v, k):
+    return jnp.where(lanes() % 8 < (2 if k == 2 else 3), rolly(v, (-4, -1, -7)[k]), 0.0)
+
+
+def merged(en, ep, ey):
+    exl = [en[0, k] + upper_end(ep[3], k) for k in range(3)]
+    exr = [en[1, k] + upper_end(ep[4], k) for k in range(3)]
+    return exl, exr, ey[0, 0] + upper_end(ep[5], 0), ey[0, 1] + upper_end(ep[5], 1)
+
+
+def completed(packs, ep):
+    exl, exr, oxl, oxr = packs
+    exl = [exl[k] + lower_end(ep[0], k) for k in range(3)]
+    exr = [exr[k] + lower_end(ep[1], k) for k in range(3)]
+    return exl, exr, oxl + lower_end(ep[2], 0), oxr + lower_end(ep[2], 1)
 
 
 def field(r, k):
@@ -505,7 +507,7 @@
     def gn(x):
         return upper.at[x]
 
-    packs = merged(en, ep, ey, False)
+    packs = merged(en, ep, ey)
     exl, exr = packs[0][0], packs[1][0]
     for x in (4, 3, 2, 1):
         pull_row(x, exl, exr, known, cot, mb, xc, xm, gn(x))
@@ -518,17 +520,17 @@
         pl.semaphore_wait(straight, 1)
         send_back()
 
+    for c in copies:
+        c.wait_send()
     for c in late[:-1]:
         c.wait_recv()
-    packs = merged(en, ep, ey, True)
+    packs = completed(packs, ep)
     exl, exr = packs[0][0], packs[1][0]
     beside[0], beside[1] = exl, exr
     pull_row(0, exl, exr, known, cot, mb, xc, xm, gn(0))
     pull_beside(packs, known, gy)
     pull_first(1, known, uck, mb, gn, gy, done.at[0])
     late[-1].wait_recv()
-    for c in copies:
-        c.wait_send()
 
 
 def finish(cot, mb, uck, rv, xc, xm, upper, gy, done, beside, out, lower, end, sems):

time: 19.3 us -> 19.3 us (level)
  no operation moved by 1% of the time
where the time goes in v8:
time: 19.3 us; the launch traced here: 19.2 us
  Pallas kernels  19.2 us (99%)
    pallas_call x1, Pallas kernels, shards(): pl.pallas_call(functools.partial(exchange, sizes), out_shape=(like(864, 1...  18.2 us
    pallas_call x1, Pallas kernels, shards(): pl.pallas_call(finish, out_shape=like(27, 8, 4, 128), in_specs=[vmem] * 1...  0.94 us

profile of v8, /device:TPU:1, one launch (start us, length us, event | category | flops | bytes accessed | tf_op | source)
XLA Modules:
  0.0 19.2 jit_solution(5073600971479602545)
XLA Ops:
  0.0 18.2 %exchange.1 = (f32[864,128]{1,0:T(8,128)S(1)}, f32[30,8,128]{2,1,0:T(8,128)S(1)}, f32[4,3,8,128]{3,2,1,0:T(8,128)S(1)}, f32[27,8,128]{2,1,0:T(8,128)S(1)}, f32[2...) custom-call(f32[27,8,4,128]{3,2,1,0:T(4,128)} %ck_hbm.1, ...), custom_call_target="tpu_custom_call" | custom-call | tf_op jit(solution)/shard_map/exchange/pallas_call | solution.py:566
  18.2 0.9 %finish.1 = f32[27,8,4,128]{3,2,1,0:T(4,128)} custom-call(f32[864,128]{1,0:T(8,128)S(1)} %get-tuple-element.15.cot, f32[30,8,128]{2,1,0:T(8,128)S(1)} %get-tuple-element.16.mb, f32[4,3,8,128]{3,2,1,0:T(8,128)S(1)} %get-tuple-element.17.uck, f32[27,8,128]{2,1,0:T(8,128)S(1)} %get-tuple-element.18.rv, f32[2,27,8,128]{3,2,1,0:T(8,128)S(1)} %get-tuple-element.19.xc, ...), custom_call_target="tpu_custom_call" | custom-call | tf_op jit(solution)/shard_map/finish/pallas_call | solution.py:594
